TPU v7x, 128 devices: a whole 4x4x4 slice. The times are simulated.
128 devices in a mesh: row: 16 (over x, z_hi, core), col: 8 (over y, z_lo).
Axes of the slice: x: 4, y: 4, z: 4 (z_hi: 2, z_lo: 2; z = z_hi * 2 + z_lo), core: 2. Of those that a mesh axis runs over, the one named last changes fastest.
Arguments:
- tile_values: bfloat16 [256, 8, 4, 128, 128], P(('row', 'col')), may hold values from 0 to 1
- tile_columns: int32 [256, 8, 4], P(('row', 'col')), may hold values from -1 to 255, as said below
- owner_map: int32 [256], replicated, may hold values from 0 to 255, as said below
- section_rows: int32 [2], replicated, may hold values from 0 to 15, as said below
Outputs:
- inflated: bfloat16 [32768, 12288], P('row', 'col')
Inputs may be any that keep to these rules, and one draw needn't show every extreme that they name: `tile_columns`: in each tile row and block-column b, the first 1 to 4 slots name distinct tile columns within b * 32 to b * 32 + 31 and the remaining slots hold -1; some tile row uses all 4 slots. A permutation of the tile rows; of the tile rows t in each aligned group of 16, exactly 1 have owner_map[t] in each block-row's range of 16 positions. `section_rows`: distinct block-rows; the last block-row is always one of them.
All inputs are finite; a program needn't handle non-finite values.
Results may differ from a plain program's by a relative error of at most 0.001.
Values may be sent and summed in bfloat16 or wider, within the bound.
A program may use at most 128 MiB of HBM per device.

v0:
```python
import functools

import jax
import jax.numpy as jnp
from jax import lax
from jax.experimental import pallas as pl
from jax.experimental.pallas import tpu as pltpu
from jax.sharding import PartitionSpec as P

TILE = 128
KB = 4
SLAB = 12
SECTIONS = 2
ROWS = 16
COLS = 8
BLOCK_COLS = 32
STRIP = TILE // COLS
ENTRIES = SECTIONS * KB
PANEL = SECTIONS * ROWS
FAST = (8, 56, 10, 16, 80)
FULL = (16, 128, 16, 32, 512)
MESH = pl.DeviceIdType.MESH
VMEM = pl.BlockSpec(memory_space=pltpu.VMEM)
SMEM = pl.BlockSpec(memory_space=pltpu.SMEM)
ANY = pl.BlockSpec(memory_space=pl.ANY)


def params(mib, **kw):
    return pltpu.CompilerParams(vmem_limit_bytes=mib << 20, **kw)


SEND, ROW_FROM, PANEL_FROM, PICKS = 0, ROWS, 2 * ROWS, 4 * ROWS


def prep_kernel(cap, owner, sections, cols, plan, inverse):
    r, c = lax.axis_index("row"), lax.axis_index("col")

    def invert(g, _):
        for j in range(ROWS):
            inverse[owner[g * ROWS + j]] = g * ROWS + j
        return 0

    lax.fori_loop(0, ROWS, invert, 0)
    secs = [sections[0], sections[1]]
    for j in range(ROWS):
        plan[SEND + (owner[r * ROWS + j] >> 4)] = j
        t = inverse[r * ROWS + j]
        plan[ROW_FROM + (t >> 4)] = t & 15
        for s in range(SECTIONS):
            t = inverse[secs[s] * ROWS + j]
            plan[PANEL_FROM + s * ROWS + (t >> 4)] = t & 15
    wanted = []
    for i in range(2):
        block = owner[r * ROWS + c * 2 + i] >> 4
        wanted.append((block == secs[0]) | (block == secs[1]))
    room = cap + 1

    def per_y(yd, _):
        for m in range(room):
            plan[PICKS + yd * room + m] = 0
        count = jnp.int32(0)
        for i in range(2):
            for z in range(2):
                b = yd * 2 + z
                for k in range(KB):
                    rel = cols[i * BLOCK_COLS + b * KB + k] - b * BLOCK_COLS
                    take = wanted[i] & (rel >= 0) & (rel < SLAB)
                    plan[PICKS + yd * room + count] = i * BLOCK_COLS + b * KB + k
                    count = jnp.minimum(count + take.astype(jnp.int32), cap)
        return 0

    lax.fori_loop(0, 4, per_y, 0)


def prep(cap, owner, sections, cols):
    return pl.pallas_call(
        functools.partial(prep_kernel, cap),
        out_shape=jax.ShapeDtypeStruct((PICKS + 4 * (cap + 1),), jnp.int32),
        in_specs=[SMEM] * 3,
        out_specs=SMEM,
        scratch_shapes=[pltpu.SMEM((ROWS * ROWS,), jnp.int32)],
    )(owner, sections, cols)


def iota(dim):
    return lax.broadcasted_iota(jnp.int32, (TILE, TILE), dim)


def picked(mask):
    return jnp.where(mask, 1.0, 0.0).astype(jnp.bfloat16)


def mm(a, b, dims=((1,), (0,))):
    return lax.dot_general(a, b, (dims, ((), ())), preferred_element_type=jnp.float32)


ROW_LEFT, ROW_HERE, ROW_THERE, ROW_KEEP = 0, 1, 2, 3
ROW_JOB, ROW_TILE, ROW_LAST, ROW_COL, ROW_OUT = 4, 5, 6, 7, 8


def vector_plan(caps, lists, owner, sections, r, c):
    cap_y, cap_left, cap_pair, cap_x, most_jobs = caps
    f32, bf, i32 = jnp.float32, jnp.bfloat16, jnp.int32
    cols = lists[...].reshape(TILE, TILE)
    line, lane = iota(0), iota(1)
    before = picked(line < lane)
    after = picked(lane < line)
    ones = jnp.ones((TILE, TILE), bf)
    same = picked(line == lane)
    nn, tn, nt = ((1,), (0,)), ((0,), (0,)), ((1,), (1,))
    small = lambda v: v.astype(f32).astype(bf)
    whole = lambda v: v.astype(i32)
    places_, blocks = [], []
    for i in range(2):
        total = jnp.zeros((TILE, TILE), f32)
        for h in range(2):
            row = jnp.broadcast_to(owner[h : h + 1, :].astype(f32), (TILE, TILE))
            total = total + mm(picked(lane + h * TILE == 2 * line + i), row.astype(bf), nt)
        places_.append(whole(total))
        blocks.append(places_[i] >> 4)
    mine = jnp.where(lane < BLOCK_COLS, blocks[0], blocks[1])
    sec0, sec1 = sections[0], sections[1]
    real = lane < 2 * BLOCK_COLS
    b = (lane & (BLOCK_COLS - 1)) >> 2
    rel = cols - b * BLOCK_COLS
    slab_mask = real & (rel >= 0) & (rel < SLAB) & ((mine == sec0) | (mine == sec1))
    slab = picked(slab_mask)
    shifted = small(jnp.where(real, cols + 1, 0))
    lane_b = (line & (BLOCK_COLS - 1)) >> 2
    row_real = line < 2 * BLOCK_COLS

    per_y = mm(slab, picked(row_real & ((lane_b >> 1) == lane)))
    per_b = small(mm(slab, picked(row_real & (lane_b == lane))))
    per_pair = mm(picked(((line >> 4) == (lane >> 4)) & ((line & 1) == (lane & 1))), per_b)
    per_x = mm(picked((line >> 5) == (lane >> 5)), per_b)
    section = lane >> 4
    target = jnp.where(section == 0, sec0, sec1) * ROWS + (lane & (ROWS - 1))
    target = jnp.where(section < SECTIONS, target, 2 * TILE + 1)
    source = jnp.where((lane >> 2) % SECTIONS == 0, sec0, sec1) >> 1
    chosen, panel_tiles = [], jnp.zeros((TILE, TILE), f32)
    for i in range(2):
        wanted = i * BLOCK_COLS + source * KB + lane % KB
        chosen.append(mm(shifted, picked((lane < ENTRIES) & (line == wanted))))
        own = (line >= i * BLOCK_COLS) & (line < (i + 1) * BLOCK_COLS)
        mine_b = small(mm(slab, picked(own & (lane_b == lane))))
        panel_tiles = panel_tiles + mm(picked(places_[i] == target), mine_b, tn)
    panel_tiles = small(panel_tiles)
    rows = jnp.zeros((TILE, TILE), f32)
    jobs = jnp.zeros((TILE, TILE), f32)
    for i in range(2):
        hits = jnp.zeros((TILE, TILE), f32)
        for e in range(ENTRIES):
            at = whole(chosen[i][:, e : e + 1]) - 1
            hits = hits + jnp.where((at == target) & (section == e // KB), 1.0, 0.0)
        hits = small(hits)
        block = picked(blocks[i] == lane)
        rows = rows + mm(block, small(mm(hits, ones)), tn)
        jobs = jobs + mm(block, small(mm(hits, panel_tiles)), tn)
    over = jnp.maximum(per_y - cap_y, rows - cap_left)
    over = jnp.maximum(over, jnp.maximum(per_pair - cap_pair, per_x - cap_x))
    over = jnp.maximum(over, jobs - most_jobs)

    got = jnp.zeros((TILE, TILE), f32)
    place = jnp.zeros((TILE, TILE), f32)
    for i in range(2):
        group = picked(((line >> 3) == lane) & (blocks[i] == r))
        got = got + mm(group, small(chosen[i]), tn)
        place = place + mm(group, small(places_[i]), tn)
    line16 = lax.broadcasted_iota(i32, (ROWS, TILE), 0)
    lane16 = lax.broadcasted_iota(i32, (ROWS, TILE), 1)
    got, place = whole(got[:ROWS]) - 1, whole(place[:ROWS]) - r * ROWS
    inner = got - jnp.where(lane16 < KB, sec0, sec1) * ROWS
    ok = (lane16 < ENTRIES) & (inner >= 0) & (inner < ROWS)
    inner = inner + (lane16 >> 2) * ROWS
    flags = picked(ok)
    spare = jnp.zeros((TILE - ROWS, TILE), bf)
    padded = jnp.concatenate([flags, spare], axis=0)
    rank = mm(padded, before) + mm(after, small(mm(padded, ones)))
    rank = jnp.where(ok, whole(rank[:ROWS]), -1)
    zero16 = jnp.zeros((ROWS, TILE), i32)
    code, left_p, left_q = zero16, zero16, zero16
    for e in range(ENTRIES):
        hit = rank[:, e : e + 1] == lane16
        code = code + jnp.where(hit, line16 * ENTRIES + e, 0)
        left_p = left_p + jnp.where(hit, place[:, e : e + 1], 0)
        left_q = left_q + jnp.where(hit, inner[:, e : e + 1] + 1, 0)
    code = code.sum(axis=0, keepdims=True)
    left_p = left_p.sum(axis=0, keepdims=True)
    left_q = left_q.sum(axis=0, keepdims=True)

    def lanes_of(column):
        wanted = (lane >> 2) * BLOCK_COLS + column * KB + lane % KB
        return picked((lane < 2 * KB) & (line == wanted))

    x, zh, y, zl = r // 4, (r // 2) % 2, c // 2, c % 2
    to_here, to_there = lanes_of(c), lanes_of(c + 1 - 2 * zl)
    of_y = slab_mask & ((b >> 1) == y)
    used = small(mm(picked(of_y), before))
    spot = ((line >> 3) & 1) * (4 * cap_y) + ((line & 7) >> 1) * cap_y
    eligible = ((line >> 4) == x * 2 + zh) & ((line & 1) == zl)

    def packed_row(key, values):
        sums = [jnp.zeros((TILE, TILE), i32) for _ in values]
        for u in range(2 * KB):
            hit = key[:, u : u + 1] == lane
            for n, value in enumerate(values):
                sums[n] = sums[n] + jnp.where(hit, value(u), 0)
        return [v.sum(axis=0, keepdims=True) for v in sums]

    def from_y(choose):
        flag = (mm(slab, choose) > 0.5) & eligible
        number = picked(flag)
        order = whole(mm(number, before) + mm(after, small(mm(number, ones))))
        at = spot + whole(mm(used, choose))
        key = jnp.where(flag, order, -1)
        return packed_row(key, [lambda u: at[:, u : u + 1]])[0]

    here, there = from_y(to_here), from_y(to_there)

    flag = mm(slab, to_here) > 0.5
    number = picked(flag)
    ahead = mm(number, before)
    rest = small(mm(number, ones))
    in_x = whole(ahead + mm(picked((lane < line) & ((line >> 5) == (lane >> 5))), rest))
    same_pair = (lane < line) & ((line >> 4) == (lane >> 4)) & ((line & 1) == (lane & 1))
    in_pair = whole(ahead + mm(picked(same_pair), rest))
    at = (((line >> 4) & 1) * 2 + (line & 1)) * cap_pair + in_pair
    key = jnp.where(flag & ((line >> 5) == x), in_x, -1)
    keep = packed_row(key, [lambda u: at[:, u : u + 1]])[0]
    key = jnp.where(flag, (line >> 5) * cap_x + in_x, -1)
    grid_col = whole(mm(shifted, to_here)) - 1 - c * BLOCK_COLS
    panel_of = []
    for i in range(2):
        q = jnp.where(blocks[i] == sec0, places_[i] - sec0 * ROWS, places_[i] - sec1 * ROWS + ROWS)
        panel_of.append(q + 1)
    right_q, right_col = packed_row(
        key, [lambda u: panel_of[u // KB], lambda u: grid_col[:, u : u + 1]]
    )

    wide = lambda row: jnp.broadcast_to(row, (TILE, TILE))
    left_q_down = whole(mm(same, small(wide(left_q)), nt))
    pair = picked((left_q_down == wide(right_q)) & (left_q_down > 0))
    number = small(mm(pair, ones))
    begin_row = whole(mm(number, before, tn))
    number_row = whole(mm(number, same, tn))
    job_of = picked((line >= begin_row) & (line < begin_row + number_row))
    begin = mm(job_of, small(mm(after, number)))
    turn = mm(job_of, small(mm(pair, before)))
    choice = (mm(job_of, pair) > 0.5) & (whole(turn) == line - whole(begin))
    choice = picked(choice)
    line8 = lax.broadcasted_iota(i32, (ROWS, TILE), 0)
    stack = jnp.where(line8 == 0, lane16, jnp.where(line8 == 1, jnp.broadcast_to(left_p, (ROWS, TILE)), 0))
    by_left = whole(mm(small(stack), job_of, nt))
    stack = jnp.where(line8 == 0, lane16, jnp.where(line8 == 1, jnp.broadcast_to(right_col, (ROWS, TILE)), 1))
    by_right = whole(mm(small(stack), choice, nt))
    job_left, job_p = by_left[0:1], by_left[1:2]
    job_tile, job_col, valid = by_right[0:1], by_right[1:2], by_right[2:3] > 0
    out = jnp.where(valid, job_p * SLAB + job_col, 255)
    out_row = wide(out)
    out_down = whole(mm(same, small(out_row), nt))
    alike = out_down == out_row
    last = jnp.where(alike & (line < lane), line, -1).max(axis=0, keepdims=True)
    later = jnp.where(alike & (line > lane), 1, 0).max(axis=0, keepdims=True)
    final = valid & (later == 0)
    made = [
        jnp.clip(code, 0, ROWS * ENTRIES - 1),
        jnp.clip(here, 0, 8 * cap_y - 1),
        jnp.clip(there, 0, 8 * cap_y - 1),
        jnp.clip(keep, 0, 4 * cap_pair - 1),
        jnp.clip(job_left, 0, cap_left - 1),
        jnp.clip(job_tile, 0, 4 * cap_x - 1),
        jnp.where(valid, jnp.clip(last, -1, most_jobs - 1), -1),
        jnp.where(final, job_col, UNUSED),
        jnp.where(final, jnp.clip(out, 0, OUT_TILES - 1), -1),
    ]
    plan = jnp.zeros((ROWS, TILE), i32)
    for n, row in enumerate(made):
        plan = jnp.where(line16 == n, jnp.broadcast_to(row, (ROWS, TILE)), plan)
    return plan, over


def spread_part(
    cap, tv, idx, sections, plan,
    strips, cand, lists,
    left_out, left_in, right_out, row_out,
    s_idx, r_idx, s_left, r_left, s_right, r_right, s_core, r_core, s_list, r_list, s_row, r_row,
    meet, on_lists, on_strips,
):
    r, c = lax.axis_index("row"), lax.axis_index("col")
    core, y, z = r % 2, c // 2, c % 2
    for i in range(2):
        for s in range(SECTIONS):
            source = sections[s] // 2
            for k in range(KB):
                for h in range(COLS):
                    left_out[h, i * ENTRIES + s * KB + k] = tv[
                        i * BLOCK_COLS + source * KB + k, h * STRIP : (h + 1) * STRIP, :
                    ]

    def pack(yd, _):
        for m in range(cap):
            right_out[yd, m] = tv[plan[PICKS + yd * (cap + 1) + m]]
        return 0

    lax.fori_loop(0, 4, pack, 0)
    lists[r, c] = idx[...]
    left_in[c] = left_out[c]
    cand[core, y] = right_out[y]
    meet()

    idx_copies, left_copies, right_copies, core_copies = [], [], [], []
    for d in range(1, COLS):
        to = (c + d) % COLS
        copy = pltpu.make_async_remote_copy(
            idx, lists.at[r, c], s_idx.at[d], r_idx.at[d], device_id={"col": to}, device_id_type=MESH
        )
        copy.start()
        idx_copies.append(copy)
    for d in range(1, COLS):
        to = (c + d) % COLS
        copy = pltpu.make_async_remote_copy(
            left_out.at[to], left_in.at[c], s_left.at[d], r_left.at[d],
            device_id={"col": to}, device_id_type=MESH,
        )
        copy.start()
        left_copies.append(copy)
    for d in (2, 1, 3):
        to = (y + d) % 4
        copy = pltpu.make_async_remote_copy(
            right_out.at[to], cand.at[core, y], s_right.at[d], r_right.at[d],
            device_id={"col": to * 2 + z}, device_id_type=MESH,
        )
        copy.start()
        right_copies.append((d, copy))

    def to_core(src, origin, d):
        copy = pltpu.make_async_remote_copy(
            src, cand.at[core, origin], s_core.at[d], r_core.at[d],
            device_id={"row": r + 1 - 2 * core}, device_id_type=MESH,
        )
        copy.start()
        core_copies.append(copy)

    to_core(right_out.at[y], y, 0)
    for copy in idx_copies:
        copy.wait_recv()
    list_copies = []
    for d in range(1, ROWS):
        to = (r + d) % ROWS
        copy = pltpu.make_async_remote_copy(
            lists.at[r], lists.at[r], s_list.at[d], r_list.at[d],
            device_id={"row": to}, device_id_type=MESH,
        )
        copy.start()
        list_copies.append(copy)
    for copy in left_copies:
        copy.wait_recv()

    def reorder(t, _):
        j = plan[SEND + t]
        for e in range(ENTRIES):
            row_out[t, e] = left_in[j // 2, (j % 2) * ENTRIES + e]
        return 0

    lax.fori_loop(0, ROWS, reorder, 0)
    strips[r] = row_out[r]
    row_copies = []
    for d in range(1, ROWS):
        to = (r + d) % ROWS
        copy = pltpu.make_async_remote_copy(
            row_out.at[to], strips.at[r], s_row.at[d], r_row.at[d],
            device_id={"row": to}, device_id_type=MESH,
        )
        copy.start()
        row_copies.append(copy)
    for copy in list_copies:
        copy.wait_recv()
    on_lists()
    for copy in row_copies:
        copy.wait_recv()
    on_strips()
    for d, copy in right_copies:
        copy.wait_recv()
        origin = (y + 4 - d) % 4
        to_core(cand.at[core, origin], origin, d)
    for copy in core_copies:
        copy.wait_recv()
    sent = [copy for _, copy in right_copies]
    return idx_copies + left_copies + sent + core_copies + list_copies + row_copies


def greet(r, c):
    barrier = pltpu.get_barrier_semaphore()
    for d in range(1, COLS):
        pl.semaphore_signal(barrier, inc=1, device_id={"col": (c + d) % COLS}, device_id_type=MESH)
    for d in range(1, ROWS):
        pl.semaphore_signal(barrier, inc=1, device_id={"row": (r + d) % ROWS}, device_id_type=MESH)
    across = {"row": (r // 4) * 4 + (r + 2) % 4, "col": c + 1 - 2 * (c % 2)}
    pl.semaphore_signal(barrier, inc=1, device_id=across, device_id_type=MESH)


def meet():
    pl.semaphore_wait(pltpu.get_barrier_semaphore(), COLS - 1 + ROWS - 1 + 1)


def spread_kernel(cap, tv, idx, sections, plan, strips, cand, lists, *scratch):
    greet(lax.axis_index("row"), lax.axis_index("col"))
    nothing = lambda: None
    started = spread_part(
        cap, tv, idx, sections, plan, strips, cand, lists, *scratch, meet, nothing, nothing
    )
    for copy in started:
        copy.wait_send()


def spread_scratch(cap):
    bf = jnp.bfloat16
    dma = pltpu.SemaphoreType.DMA
    return (
        [
            pltpu.VMEM((COLS, 2 * ENTRIES, STRIP, TILE), bf),
            pltpu.VMEM((COLS, 2 * ENTRIES, STRIP, TILE), bf),
            pltpu.VMEM((4, cap, TILE, TILE), bf),
            pltpu.VMEM((ROWS, ENTRIES, STRIP, TILE), bf),
        ]
        + [dma((COLS,))] * 8
        + [dma((ROWS,))] * 4
    )


def spread(cap, collective_id, tv, idx, sections, plan):
    bf = jnp.bfloat16
    return pl.pallas_call(
        functools.partial(spread_kernel, cap),
        out_shape=(
            jax.ShapeDtypeStruct((ROWS, ENTRIES, STRIP, TILE), bf),
            jax.ShapeDtypeStruct((2, 4, cap, TILE, TILE), bf),
            jax.ShapeDtypeStruct((ROWS, COLS, 1, TILE), jnp.int32),
        ),
        in_specs=[VMEM, VMEM, SMEM, SMEM],
        out_specs=(VMEM,) * 3,
        scratch_shapes=spread_scratch(cap),
        compiler_params=params(20, collective_id=collective_id, has_side_effects=True),
    )(tv, idx, sections, plan)


OUT_TILES = ROWS * SLAB
UNUSED = ROWS - 1


def places(caps):
    cap_y, cap_left, cap_pair, cap_x, jobs = caps
    sizes = (
        ("left", cap_left + 8), ("here", cap_pair + 8), ("there", cap_pair + 8), ("keep", cap_x + 8),
        ("job_left", jobs + 8), ("job_right", jobs + 8), ("job_last", jobs + 8), ("job_col", jobs + 8),
        ("out", OUT_TILES), ("slot", OUT_TILES), ("touched", 8),
    )
    at, found = 0, {}
    for name, size in sizes:
        found[name] = at
        at += size
    return found, at


class Part:
    def __init__(self, ref, base):
        self.ref, self.base = ref, base

    def __getitem__(self, i):
        return self.ref[self.base + i]

    def __setitem__(self, i, value):
        self.ref[self.base + i] = value


def lists_kernel(
    caps, lists, owner, sections, plan, made, blank,
    zeros, row_left, inner_left, start, count, col_right, zero_sem,
):
    cap_y, cap_left, cap_pair, cap_x, jobs = caps
    zeros[...] = jnp.zeros_like(zeros)
    for p in range(ROWS):
        pltpu.make_async_copy(zeros, blank.at[pl.ds(p * TILE, TILE)], zero_sem.at[p]).start()
    part = {name: Part(made, base) for name, base in places(caps)[0].items()}
    keep_left, here, there, keep = part["left"], part["here"], part["there"], part["keep"]
    job_left, job_right = part["job_left"], part["job_right"]
    job_last, job_col = part["job_last"], part["job_col"]
    out_of, slot_of = part["out"], part["slot"]
    row_from, panel_from = Part(plan, ROW_FROM), Part(plan, PANEL_FROM)
    r, c = lax.axis_index("row"), lax.axis_index("col")
    x, zh = r >> 2, (r >> 1) & 1
    y, zl = c >> 1, c & 1
    secs = [sections[0], sections[1]]
    for m in range(cap_pair):
        here[m] = 0
        there[m] = 0
    for m in range(cap_x):
        keep[m] = 0

    def clear(m, _):
        for u in range(8):
            keep_left[m * 8 + u] = 0
        return 0

    lax.fori_loop(0, cap_left // 8, clear, 0)

    def left(g, n):
        j = row_from[g]
        line = g * COLS + (j >> 1)
        base = (j & 1) * BLOCK_COLS
        p = owner[g * ROWS + j] - r * ROWS
        for s in range(SECTIONS):
            for k in range(KB):
                rel = lists[line, base + (secs[s] >> 1) * KB + k] - secs[s] * ROWS
                keep_left[n] = g * ENTRIES + s * KB + k
                row_left[n] = p
                inner_left[n] = s * ROWS + rel
                n = n + ((rel >= 0) & (rel < ROWS)).astype(jnp.int32)
        return n

    left_count = lax.fori_loop(0, ROWS, left, jnp.int32(0))

    def ordered(g):
        a, b = panel_from[g], panel_from[ROWS + g]
        swap = (b < a).astype(jnp.int32)
        return ((swap, jnp.minimum(a, b)), (1 - swap, jnp.maximum(a, b)))

    def pairs(k2, carry):
        n_here, n_there = carry
        g = x * 4 + zh * 2 + k2
        used = jnp.int32(0)
        before = jnp.int32(-1)
        for s, j in ordered(g):
            source = j >> 1
            used = jnp.where(source == before, used, 0)
            before = source
            line = g * COLS + source
            base = (j & 1) * BLOCK_COLS
            near = (source & 1) == zl
            spot = k2 * 4 * cap_y + (source >> 1) * cap_y
            for z in range(2):
                mine = zl == z
                for k in range(KB):
                    b = y * 2 + z
                    rel = lists[line, base + b * KB + k] - b * BLOCK_COLS
                    ok = (rel >= 0) & (rel < SLAB)
                    take_here = (ok & near & mine).astype(jnp.int32)
                    take_there = (ok & near & jnp.logical_not(mine)).astype(jnp.int32)
                    at = jnp.minimum(spot + used, 8 * cap_y - 1)
                    here[n_here] = at
                    there[n_there] = at
                    n_here = n_here + take_here
                    n_there = n_there + take_there
                    used = used + ok.astype(jnp.int32)
        return n_here, n_there

    lax.fori_loop(0, 2, pairs, (jnp.int32(0), jnp.int32(0)))

    def per_x(xs, _):
        def per_zh(zs, n):
            def per_core(k2, carry):
                n, seen0, seen1 = carry
                g = xs * 4 + zs * 2 + k2
                for s, j in ordered(g):
                    source = j >> 1
                    sec = jnp.where(s == 0, secs[0], secs[1])
                    q = s * ROWS + owner[g * ROWS + j] - sec * ROWS
                    line = g * COLS + source
                    base = (j & 1) * BLOCK_COLS + c * KB
                    odd = source & 1
                    first = n
                    for k in range(KB):
                        rel = lists[line, base + k] - c * BLOCK_COLS
                        take = ((rel >= 0) & (rel < SLAB)).astype(jnp.int32)
                        seen = jnp.where(odd == 0, seen0, seen1)
                        at = jnp.minimum((zs * 2 + odd) * cap_pair + seen, 4 * cap_pair - 1)
                        col_right[xs * (cap_x + 1) + n] = rel
                        keep[jnp.where(xs == x, n, cap_x)] = at
                        n = n + take
                        seen0 = seen0 + take * (1 - odd)
                        seen1 = seen1 + take * odd
                    start[q] = xs * (cap_x + 1) + first
                    count[q] = n - first
                return n, seen0, seen1

            return lax.fori_loop(0, 2, per_core, (n, jnp.int32(0), jnp.int32(0)))[0]

        lax.fori_loop(0, 2, per_zh, jnp.int32(0))
        return 0

    lax.fori_loop(0, 4, per_x, 0)

    def no_slot(o, _):
        for u in range(16):
            slot_of[o * 16 + u] = -1
        return 0

    lax.fori_loop(0, OUT_TILES // 16, no_slot, 0)

    def no_job(n, _):
        for u in range(8):
            job_left[n * 8 + u] = 0
            job_right[n * 8 + u] = 0
            job_last[n * 8 + u] = -1
            job_col[n * 8 + u] = UNUSED
        return 0

    lax.fori_loop(0, jobs // 8, no_job, 0)

    def per_left(m, carry):
        first = row_left[m] * SLAB
        q = inner_left[m]
        begin = start[q]

        def per_right(t, carry):
            n, touched = carry
            at = begin + t
            col = col_right[at]
            o = first + col
            last = slot_of[o]
            fresh = last < 0
            job_left[n] = m
            job_right[n] = at - at // (cap_x + 1)
            job_last[n] = last
            job_col[n] = col
            job_col[jnp.where(fresh, jobs + 1, last)] = UNUSED
            slot_of[o] = n
            out_of[jnp.where(fresh, touched, OUT_TILES - 1)] = jnp.where(
                fresh, o, out_of[OUT_TILES - 1]
            )
            return n + 1, touched + fresh.astype(jnp.int32)

        return lax.fori_loop(0, count[q], per_right, carry)

    _, touched = lax.fori_loop(0, left_count, per_left, (jnp.int32(0), jnp.int32(0)))
    part["touched"][0] = touched
    for p in range(ROWS):
        pltpu.make_async_copy(zeros, blank.at[pl.ds(p * TILE, TILE)], zero_sem.at[p]).wait()


def make_lists(caps, lists, owner, sections, plan):
    cap_y, cap_left, cap_pair, cap_x, jobs = caps
    smem = lambda n: pltpu.SMEM((n,), jnp.int32)
    return pl.pallas_call(
        functools.partial(lists_kernel, caps),
        out_shape=(
            jax.ShapeDtypeStruct((places(caps)[1],), jnp.int32),
            jax.ShapeDtypeStruct((ROWS * TILE, SLAB * TILE), jnp.bfloat16),
        ),
        in_specs=[SMEM] * 4,
        out_specs=(SMEM, ANY),
        scratch_shapes=[
            pltpu.VMEM((TILE, SLAB * TILE), jnp.bfloat16),
            smem(cap_left + 8), smem(cap_left + 8), smem(PANEL), smem(PANEL), smem(4 * (cap_x + 1)),
            pltpu.SemaphoreType.DMA((ROWS,)),
        ],
        compiler_params=params(4),
    )(lists, owner, sections, plan)


UNROLL = 8


def gather_part(caps, keep_left, here, there, keep, strips, cand, left, right, held, other, send, recv):
    cap_y, cap_left, cap_pair, cap_x, jobs = caps
    r, c = lax.axis_index("row"), lax.axis_index("col")
    k = r % 2
    x, y = r // 4, c // 2
    me = ((r // 2) % 2) * 2 + c % 2
    cz = c + 1 - 2 * (c % 2)
    rz = (r // 4) * 4 + (r + 2) % 4
    cut = cap_left * 11 // 14
    zp, zh, zx = {"col": cz}, {"row": rz}, {"row": rz, "col": cz}
    yn, yb = {"col": (c + 2) % COLS}, {"col": (c + COLS - 2) % COLS}
    core = {"row": r + 1 - 2 * k}
    xn, xb = {"row": (r + 4) % ROWS}, {"row": (r + ROWS - 4) % ROWS}
    half, part = cap_pair // 2, cap_x // 2

    def pack_left(m, _):
        for u in range(4):
            e = keep_left[m * 4 + u]
            left[c, m * 4 + u] = strips[e // ENTRIES, e % ENTRIES]
        return 0

    lax.fori_loop(0, cap_left // 4, pack_left, 0)

    started, done = [], []

    def push(src, dst, to):
        n = len(started)
        copy = pltpu.make_async_remote_copy(
            src, dst, send.at[n], recv.at[n], device_id=to, device_id_type=MESH
        )
        copy.start()
        started.append(copy)
        return copy

    def go(origin, a, b, to):
        piece = left.at[origin, pl.ds(a, b - a)]
        return push(piece, piece, to)

    def gx(origin, a, b, to):
        piece = right.at[origin, k, pl.ds(a, b - a)]
        return push(piece, piece, to)

    def arrived(copy):
        copy.wait_recv()
        done.append(copy)

    end = cap_left
    a_mid, b_mid = cut // 2, (cut + end) // 2
    c_m, c_p, c_o = (c + COLS - 2) % COLS, (c + 2) % COLS, (c + 4) % COLS
    z_m, z_p = (cz + COLS - 2) % COLS, (cz + 2) % COLS
    x_m, x_p, x_o = (x + 3) % 4, (x + 1) % 4, (x + 2) % 4
    z_of_p, z_of_h = (me // 2) * 2 + (me + 1) % 2, (me + 2) % 4
    z_of_x = (z_of_p + 2) % 4

    k1 = go(c, 0, cut, zp)
    k2 = go(c, 0, cut, yn)
    k3 = go(c, 0, cut, yb)
    k10 = go(c, cut, end, yn)
    k11 = go(c, cut, end, yb)
    k12 = go(c, cut, end, zp)
    yield
    for m in range(half):
        e = there[k * half + m]
        other[m] = cand[e // (4 * cap_y), (e // cap_y) % 4, e % cap_y]
    for m in range(cap_pair):
        e = here[m]
        held[me, m // half, m % half] = cand[e // (4 * cap_y), (e // cap_y) % 4, e % cap_y]

    s1 = push(other, held.at[me, k], zp)
    s2 = push(other, held.at[me, k], zx)
    s3 = push(held.at[me, k], held.at[me, k], zh)
    arrived(s1)
    t1 = push(held.at[z_of_p, k], held.at[z_of_p, k], core)
    arrived(s2)
    t2 = push(held.at[z_of_x, k], held.at[z_of_x, k], core)
    arrived(s3)
    t3 = push(held.at[z_of_h, k], held.at[z_of_h, k], core)
    arrived(k2)
    k6 = go(c_m, 0, a_mid, yn)
    arrived(k3)
    k7 = go(c_p, a_mid, cut, yb)
    arrived(k1)
    k4 = go(cz, 0, cut, yn)
    k5 = go(cz, 0, cut, yb)
    arrived(t1)
    arrived(t2)
    arrived(t3)
    for m in range(cap_x):
        e = keep[m]
        right[x, m // part, m % part] = held[e // cap_pair, (e // half) % 2, e % half]
    u1 = gx(x, 0, part, xn)
    u2 = gx(x, 0, part, xb)
    arrived(k10)
    k13 = go(c_m, cut, b_mid, yn)
    k14 = go(c_m, cut, end, zp)
    arrived(k11)
    k15 = go(c_p, b_mid, end, yb)
    k16 = go(c_p, cut, end, zp)
    arrived(u1)
    u3 = gx(x_m, 0, part // 2, xn)
    u4 = gx(x_m, 0, part, core)
    arrived(u2)
    u5 = gx(x_p, part // 2, part, xb)
    u6 = gx(x_p, 0, part, core)
    arrived(k4)
    k8 = go(z_m, 0, a_mid, yn)
    arrived(k5)
    k9 = go(z_p, a_mid, cut, yb)
    arrived(k13)
    k17 = go(c_o, cut, b_mid, zp)
    arrived(k15)
    k18 = go(c_o, b_mid, end, zp)
    arrived(u3)
    u7 = gx(x_o, 0, part // 2, core)
    arrived(u5)
    u8 = gx(x_o, part // 2, part, core)
    for copy in started:
        if not any(copy is seen for seen in done):
            copy.wait_recv()
    yield started


def product_part(
    caps, job_left, job_right, job_last, job_col, left, right, sums, totals, rows, parts,
    total_send, total_recv,
):
    cap_y, cap_left, cap_pair, cap_x, jobs = caps
    r = lax.axis_index("row")
    part = cap_x // 2
    rows[...] = jnp.zeros_like(rows)
    line = lax.broadcasted_iota(jnp.int32, (ROWS, TILE), 0)

    def multiply(g, _):
        results = []
        for u in range(UNROLL):
            n = g * UNROLL + u
            a = left[:, job_left[n]].reshape(TILE, TILE)
            e = job_right[n]
            b = right[e // cap_x, (e // part) % 2, e % part]
            results.append(jnp.dot(a, b, preferred_element_type=jnp.float32))
        added = jnp.zeros((ROWS, TILE), jnp.float32)
        for u in range(UNROLL):
            n = g * UNROLL + u
            last = job_last[n]
            old = sums[jnp.maximum(last, 0)]
            value = results[u] + jnp.where(last >= 0, old, 0.0)
            sums[n] = value
            square = (value * value).reshape(TILE // 8, 8, TILE).sum(axis=0)
            square = square.sum(axis=0, keepdims=True)
            added = added + jnp.where(line == job_col[n], square, 0.0)
        rows[...] += added
        return 0

    lax.fori_loop(0, jobs // UNROLL, multiply, 0)
    parts[r] = rows[...]
    copies = []
    for d in range(1, ROWS):
        copy = pltpu.make_async_remote_copy(
            rows, parts.at[r], total_send.at[d], total_recv.at[d],
            device_id={"row": (r + d) % ROWS}, device_id_type=MESH,
        )
        copy.start()
        copies.append(copy)
    for copy in copies:
        copy.wait_recv()
    totals[...] = parts[...].sum(axis=0)
    return copies


def multiply_kernel(
    caps, strips, cand, plan, sums, totals,
    left, right, held, other, rows, parts, send, recv, total_send, total_recv,
):
    greet(lax.axis_index("row"), lax.axis_index("col"))
    found = {name: Part(plan, base) for name, base in places(caps)[0].items()}
    meet()
    steps = gather_part(
        caps, found["left"], found["here"], found["there"], found["keep"],
        strips, cand, left, right, held, other, send, recv,
    )
    next(steps)
    started = next(steps)
    started += product_part(
        caps, found["job_left"], found["job_right"], found["job_last"], found["job_col"],
        left, right, sums, totals, rows, parts, total_send, total_recv,
    )
    for copy in started:
        copy.wait_send()


COPIES = 32


def multiply_scratch(caps):
    cap_y, cap_left, cap_pair, cap_x, jobs = caps
    bf, f32 = jnp.bfloat16, jnp.float32
    dma = pltpu.SemaphoreType.DMA
    return (
        [
            pltpu.VMEM((COLS, cap_left, STRIP, TILE), bf),
            pltpu.VMEM((4, 2, cap_x // 2, TILE, TILE), bf),
            pltpu.VMEM((4, 2, cap_pair // 2, TILE, TILE), bf),
            pltpu.VMEM((cap_pair // 2, TILE, TILE), bf),
            pltpu.VMEM((ROWS, TILE), f32),
            pltpu.VMEM((ROWS, ROWS, TILE), f32),
        ]
        + [dma((COPIES,))] * 2
        + [dma((ROWS,))] * 2
    )


def multiply(caps, collective_id, strips, cand, plan):
    jobs, f32 = caps[4], jnp.float32
    mib = 24 + jobs * TILE * TILE * 4 // (1 << 20)
    return pl.pallas_call(
        functools.partial(multiply_kernel, caps),
        out_shape=(
            jax.ShapeDtypeStruct((jobs, TILE, TILE), f32),
            jax.ShapeDtypeStruct((ROWS, TILE), f32),
        ),
        in_specs=[VMEM, VMEM, SMEM],
        out_specs=(VMEM, VMEM),
        scratch_shapes=multiply_scratch(caps),
        compiler_params=params(mib, collective_id=collective_id, has_side_effects=True),
    )(strips, cand, plan)


class Row:
    def __init__(self, ref, row):
        self.ref, self.row = ref, row

    def __getitem__(self, i):
        return self.ref[self.row, i]


def whole_kernel(
    caps, tv, idx, owner, sections, plan,
    sums, totals, blank, made, over,
    strips, cand, lists, zeros, scalars, zero_sem, plan_sem, *scratch,
):
    r, c = lax.axis_index("row"), lax.axis_index("col")
    greet(r, c)
    zeros[...] = jnp.zeros_like(zeros)
    clears = [
        pltpu.make_async_copy(zeros, blank.at[pl.ds(p * TILE, TILE)], zero_sem.at[p])
        for p in range(ROWS)
    ]
    first, second = scratch[:16], scratch[16:]
    left, right, held, other, rows, parts, send, recv, total_send, total_recv = second
    row = lambda n: Row(scalars, n)
    steps = gather_part(
        caps, row(ROW_LEFT), row(ROW_HERE), row(ROW_THERE), row(ROW_KEEP),
        strips, cand, left, right, held, other, send, recv,
    )

    def on_lists():
        found, excess = vector_plan(caps, lists, owner, sections, r, c)
        made[...] = found
        over[...] = excess
        move = pltpu.make_async_copy(made, scalars, plan_sem)
        move.start()
        for copy in clears:
            copy.start()
        move.wait()

    started = spread_part(
        caps[0], tv, idx, sections, plan, strips, cand, lists, *first,
        meet, on_lists, lambda: next(steps),
    )
    started = started + next(steps)
    started += product_part(
        caps, row(ROW_JOB), row(ROW_TILE), row(ROW_LAST), row(ROW_COL),
        left, right, sums, totals, rows, parts, total_send, total_recv,
    )
    for copy in started:
        copy.wait_send()
    for copy in clears:
        copy.wait()


def whole(caps, collective_id, tv, idx, owner, sections, plan):
    bf, f32, i32 = jnp.bfloat16, jnp.float32, jnp.int32
    dma = pltpu.SemaphoreType.DMA
    return pl.pallas_call(
        functools.partial(whole_kernel, caps),
        out_shape=(
            jax.ShapeDtypeStruct((caps[4], TILE, TILE), f32),
            jax.ShapeDtypeStruct((ROWS, TILE), f32),
            jax.ShapeDtypeStruct((ROWS * TILE, SLAB * TILE), bf),
            jax.ShapeDtypeStruct((ROWS, TILE), i32),
            jax.ShapeDtypeStruct((TILE, TILE), f32),
        ),
        in_specs=[VMEM, VMEM, VMEM, SMEM, SMEM],
        out_specs=(VMEM, VMEM, ANY, VMEM, VMEM),
        scratch_shapes=[
            pltpu.VMEM((ROWS, ENTRIES, STRIP, TILE), bf),
            pltpu.VMEM((2, 4, caps[0], TILE, TILE), bf),
            pltpu.VMEM((ROWS, COLS, 1, TILE), i32),
            pltpu.VMEM((TILE, SLAB * TILE), bf),
            pltpu.SMEM((ROWS, TILE), i32),
            dma((ROWS,)),
            dma,
        ]
        + spread_scratch(caps[0])
        + multiply_scratch(caps),
        compiler_params=params(40, collective_id=collective_id, has_side_effects=True),
    )(tv, idx, owner, sections, plan)


def write_listed_kernel(jobs, sums, blank, plan, totals, out, block, factor, out_sem):
    count = float(ROWS * ROWS * TILE)
    factor[...] = count / (totals[...] + 1e-06)

    def place(n):
        o = plan[ROW_OUT, n]
        p = jnp.maximum(o, 0) // SLAB
        col = jnp.maximum(o, 0) - p * SLAB
        row = pl.ds(pl.multiple_of(p * TILE, TILE), TILE)
        lanes = pl.ds(pl.multiple_of(col * TILE, TILE), TILE)
        return o, col, pltpu.make_async_copy(block.at[n], out.at[row, lanes], out_sem)

    def scale(n, _):
        o, col, copy = place(n)

        @pl.when(o >= 0)
        def _():
            value = sums[n]
            block[n] = (value * value * factor[pl.ds(col, 1), :]).astype(jnp.bfloat16)
            copy.start()

        return 0

    lax.fori_loop(0, jobs, scale, 0)

    def drain(n, _):
        o, _, copy = place(n)

        @pl.when(o >= 0)
        def _():
            copy.wait()

        return 0

    lax.fori_loop(0, jobs, drain, 0)


def write_listed(jobs, sums, blank, plan, totals):
    return pl.pallas_call(
        functools.partial(write_listed_kernel, jobs),
        out_shape=jax.ShapeDtypeStruct((ROWS * TILE, SLAB * TILE), jnp.bfloat16),
        in_specs=[VMEM, ANY, SMEM, VMEM],
        out_specs=ANY,
        input_output_aliases={1: 0},
        scratch_shapes=[
            pltpu.VMEM((jobs, TILE, TILE), jnp.bfloat16),
            pltpu.VMEM((ROWS, TILE), jnp.float32),
            pltpu.SemaphoreType.DMA,
        ],
        compiler_params=params(12),
    )(sums, blank, plan, totals)


def write_kernel(at, sums, blank, plan, totals, out, block, factor, out_sem):
    touched = plan[at["touched"]]
    count = float(ROWS * ROWS * TILE)
    factor[...] = count / (totals[...] + 1e-06)

    def place(i):
        o = plan[at["out"] + i]
        p = o // SLAB
        col = o - p * SLAB
        row = pl.ds(pl.multiple_of(p * TILE, TILE), TILE)
        lanes = pl.ds(pl.multiple_of(col * TILE, TILE), TILE)
        return o, col, pltpu.make_async_copy(block.at[i], out.at[row, lanes], out_sem)

    def scale(i, _):
        o, col, copy = place(i)
        value = sums[plan[at["slot"] + o]]
        block[i] = (value * value * factor[pl.ds(col, 1), :]).astype(jnp.bfloat16)
        copy.start()
        return 0

    lax.fori_loop(0, touched, scale, 0)

    def drain(i, _):
        place(i)[2].wait()
        return 0

    lax.fori_loop(0, touched, drain, 0)


def write(caps, sums, blank, plan, totals):
    jobs = caps[4]
    mib = 10 + jobs * TILE * TILE * 4 // (1 << 20)
    return pl.pallas_call(
        functools.partial(write_kernel, places(caps)[0]),
        out_shape=jax.ShapeDtypeStruct((ROWS * TILE, SLAB * TILE), jnp.bfloat16),
        in_specs=[VMEM, ANY, SMEM, VMEM],
        out_specs=ANY,
        input_output_aliases={1: 0},
        scratch_shapes=[
            pltpu.VMEM((OUT_TILES, TILE, TILE), jnp.bfloat16),
            pltpu.VMEM((ROWS, TILE), jnp.float32),
            pltpu.SemaphoreType.DMA,
        ],
        compiler_params=params(mib),
    )(sums, blank, plan, totals)


def per_device(tile_values, tile_columns, owner_map, section_rows):
    flat = tile_columns.reshape(-1)
    idx = jnp.pad(flat, (0, TILE - flat.shape[0])).reshape(1, TILE)
    tv = tile_values.reshape(2 * COLS * KB, TILE, TILE)
    owner_rows = owner_map.reshape(2, TILE)

    def full():
        plan = prep(FULL[0], owner_map, section_rows, flat)
        strips, cand, lists = spread(FULL[0], 2, tv, idx, section_rows, plan)
        made, blank = make_lists(
            FULL, lists.reshape(ROWS * COLS, TILE), owner_map, section_rows, plan
        )
        sums, totals = multiply(FULL, 3, strips, cand, made)
        return write(FULL, sums, blank, made, totals)

    plan = prep(FAST[0], owner_map, section_rows, flat)
    *got, over = whole(FAST, 0, tv, idx, owner_rows, section_rows, plan)

    def packed(sums, totals, blank, made):
        return write_listed(FAST[4], sums, blank, made, totals)

    return lax.cond(jnp.max(over) > 0, lambda *_: full(), packed, *got)


def solution(mesh):
    both = ("row", "col")
    in_specs = (P(both, None, None, None, None), P(both, None, None), P(), P())
    return jax.shard_map(
        per_device, mesh=mesh, in_specs=in_specs, out_specs=P("row", "col"), check_vma=False
    )
```

profile of v0, /device:TPU:1, one launch (start us, length us, event | category | flops | bytes accessed | tf_op | source)
XLA Modules:
  0.0 90.3 jit_solution(15691585054834600575)
XLA Ops:
  0.0 0.8 copy.10
  0.8 0.1 reshape.16.cols
  0.9 2.0 %shard_map.48.plan = s32[100]{0:T(128)} custom-call(s32[256]{0:T(256)} %owner.1, s32[2]{0:T(128)} %sections.3, s32[64]{0:T(128)S(1)} %reshape.16.cols), custom_call_target="tpu_custom_call" | custom-call | tf_op jit(solution)/shard_map/pallas_call | solution.py:76
  2.8 0.0 copy-start.6
  2.9 0.6 copy-done.6
  3.5 74.1 %shard_map.49 = (f32[80,128,128]{2,1,0:T(8,128)}, f32[16,128]{1,0:T(8,128)S(1)}, bf16[2048,1536]{1,0:T(8,128)(2,1)}, s32[16,128]{1,0:T(8,128)S(1)}, f32[128,128]{1,0:T(8,128)S(1)}) custom-call(bf16[64,128,128]{2,1,0:T(8,128)(2,1)} %bitcast.6, s32[1,128]{1,0:T(1,128)S(1)} %pad_bitcast_fusion.idx, s32[2,128]{1,0:T(2,128)} %bitcast.8, s32[2]{0:T(128)} %sections.3, ...), custom_call_target="tpu_custom_call" | custom-call | tf_op jit(solution)/shard_map/pallas_call | solution.py:947
  77.7 0.6 reduce_max.9
  78.9 5.5 %conditional.1 = (bf16[2048,1536]{1,0:T(8,128)(2,1)}) conditional(s32[]{:T(128)} %convert_element_type.3, (f32[80,128,128]{2,1,0:T(8,128)}, bf16[2048,1536]{1,0:T(8,128)(2,1)}, s32[16,128]{1,0:T(8,128)S(1)}, f32[16,128]{1,0:T(8,128)S(1)}) %tuple.11, (s32[256]{0:T(256)}, s32[2]{0:T(128)}, s32[64]{0:T(128)S(1)}, bf16[64,128,128]{2,1,0:T(8,128)(2,1)}, ...), branch_computations={%region_1.2_spmd, %region_2.3_spmd} | conditional | bytes 44161548 | solution.py:1094
  78.9 5.4 %branch_0_fun.1 = bf16[2048,1536]{1,0:T(8,128)(2,1)} custom-call(f32[80,128,128]{2,1,0:T(8,128)} %get-tuple-element.26.sums, bf16[2048,1536]{1,0:T(8,128)(2,1)} %get-tuple-element.27.blank, s32[16,128]{1,0:T(8,128)S(1)} %get-tuple-element.28.plan, f32[16,128]{1,0:T(8,128)S(1)} %get-tuple-element.29.totals), custom_call_target="tpu_custom_call", output_to_operand_aliasing={{}: (1, {})} | custom-call | tf_op jit(solution)/shard_map/cond/branch_0_fun/pallas_call | solution.py:1011
  84.4 5.9 %copy.16 = bf16[2048,1536]{1,0:T(8,128)(2,1)} copy(bf16[2048,1536]{1,0:T(8,128)(2,1)} %get-tuple-element.52) | data formatting | bytes 12582912
  (1 shorter events, 0.0 us)
Async XLA Ops:
  2.8 0.7 copy-start.6
where the time goes:
time: 91.1 us; the launch traced here: 90.3 us
  Pallas kernels  81.6 us (90%)
  local copies, waits for them, and re-layouts  7.4 us (8%)
    pallas_call x1, Pallas kernels, whole(): pl.pallas_call(functools.partial(whole_kernel, caps), out_shape=(jax.Shap...  74.1 us
    unnamed x4, local copies, waits for them, and re-layouts  7.31 us
    pallas_call x1, Pallas kernels, write_listed(): pl.pallas_call(functools.partial(write_listed_kernel, jobs), out_shape=ja...  5.43 us
    pallas_call x1, Pallas kernels, prep(): pl.pallas_call(functools.partial(prep_kernel, cap), out_shape=jax.ShapeDt...  1.97 us

commit v1 on v0

--- a/solution.py
+++ b/solution.py
@@ -17,12 +17,13 @@
 STRIP = TILE // COLS
 ENTRIES = SECTIONS * KB
 PANEL = SECTIONS * ROWS
-FAST = (8, 56, 10, 16, 80)
-FULL = (16, 128, 16, 32, 512)
+FAST = (8, 56, 6, 16, 80)
+FULL = (16, 128, 8, 32, 512)
 MESH = pl.DeviceIdType.MESH
 VMEM = pl.BlockSpec(memory_space=pltpu.VMEM)
 SMEM = pl.BlockSpec(memory_space=pltpu.SMEM)
 ANY = pl.BlockSpec(memory_space=pl.ANY)
+HBM = pl.BlockSpec(memory_space=pltpu.HBM)
 
 
 def params(mib, **kw):
@@ -32,8 +33,15 @@
 SEND, ROW_FROM, PANEL_FROM, PICKS = 0, ROWS, 2 * ROWS, 4 * ROWS
 
 
-def prep_kernel(cap, owner, sections, cols, plan, inverse):
+def prep_kernel(cap, owner, sections, cols, plan, blank, inverse, zeros, zero_sem):
     r, c = lax.axis_index("row"), lax.axis_index("col")
+    zeros[...] = jnp.zeros_like(zeros)
+    clears = [
+        pltpu.make_async_copy(zeros, blank.at[pl.ds(p * TILE, TILE)], zero_sem.at[p])
+        for p in range(ROWS)
+    ]
+    for copy in clears:
+        copy.start()
 
     def invert(g, _):
         for j in range(ROWS):
@@ -70,15 +78,25 @@
         return 0
 
     lax.fori_loop(0, 4, per_y, 0)
+    for copy in clears:
+        copy.wait()
 
 
 def prep(cap, owner, sections, cols):
     return pl.pallas_call(
         functools.partial(prep_kernel, cap),
-        out_shape=jax.ShapeDtypeStruct((PICKS + 4 * (cap + 1),), jnp.int32),
+        out_shape=(
+            jax.ShapeDtypeStruct((PICKS + 4 * (cap + 1),), jnp.int32),
+            jax.ShapeDtypeStruct((ROWS * TILE, SLAB * TILE), jnp.bfloat16),
+        ),
         in_specs=[SMEM] * 3,
-        out_specs=SMEM,
-        scratch_shapes=[pltpu.SMEM((ROWS * ROWS,), jnp.int32)],
+        out_specs=(SMEM, ANY),
+        scratch_shapes=[
+            pltpu.SMEM((ROWS * ROWS,), jnp.int32),
+            pltpu.VMEM((TILE, SLAB * TILE), jnp.bfloat16),
+            pltpu.SemaphoreType.DMA((ROWS,)),
+        ],
+        compiler_params=params(4),
     )(owner, sections, cols)
 
 
@@ -131,7 +149,7 @@
 
     per_y = mm(slab, picked(row_real & ((lane_b >> 1) == lane)))
     per_b = small(mm(slab, picked(row_real & (lane_b == lane))))
-    per_pair = mm(picked(((line >> 4) == (lane >> 4)) & ((line & 1) == (lane & 1))), per_b)
+    per_pair = mm(picked(((line >> 3) == (lane >> 3)) & ((line & 1) == (lane & 1))), per_b)
     per_x = mm(picked((line >> 5) == (lane >> 5)), per_b)
     section = lane >> 4
     target = jnp.where(section == 0, sec0, sec1) * ROWS + (lane & (ROWS - 1))
@@ -192,12 +210,12 @@
         wanted = (lane >> 2) * BLOCK_COLS + column * KB + lane % KB
         return picked((lane < 2 * KB) & (line == wanted))
 
-    x, zh, y, zl = r // 4, (r // 2) % 2, c // 2, c % 2
+    x, y, zl = r // 4, c // 2, c % 2
     to_here, to_there = lanes_of(c), lanes_of(c + 1 - 2 * zl)
     of_y = slab_mask & ((b >> 1) == y)
     used = small(mm(picked(of_y), before))
-    spot = ((line >> 3) & 1) * (4 * cap_y) + ((line & 7) >> 1) * cap_y
-    eligible = ((line >> 4) == x * 2 + zh) & ((line & 1) == zl)
+    spot = ((line & 7) >> 1) * cap_y
+    eligible = ((line >> 3) == r) & ((line & 1) == zl)
 
     def packed_row(key, values):
         sums = [jnp.zeros((TILE, TILE), i32) for _ in values]
@@ -222,9 +240,9 @@
     ahead = mm(number, before)
     rest = small(mm(number, ones))
     in_x = whole(ahead + mm(picked((lane < line) & ((line >> 5) == (lane >> 5))), rest))
-    same_pair = (lane < line) & ((line >> 4) == (lane >> 4)) & ((line & 1) == (lane & 1))
+    same_pair = (lane < line) & ((line >> 3) == (lane >> 3)) & ((line & 1) == (lane & 1))
     in_pair = whole(ahead + mm(picked(same_pair), rest))
-    at = (((line >> 4) & 1) * 2 + (line & 1)) * cap_pair + in_pair
+    at = ((((line >> 4) & 1) * 2 + (line & 1)) * 2 + ((line >> 3) & 1)) * cap_pair + in_pair
     key = jnp.where(flag & ((line >> 5) == x), in_x, -1)
     keep = packed_row(key, [lambda u: at[:, u : u + 1]])[0]
     key = jnp.where(flag, (line >> 5) * cap_x + in_x, -1)
@@ -264,9 +282,9 @@
     final = valid & (later == 0)
     made = [
         jnp.clip(code, 0, ROWS * ENTRIES - 1),
-        jnp.clip(here, 0, 8 * cap_y - 1),
-        jnp.clip(there, 0, 8 * cap_y - 1),
-        jnp.clip(keep, 0, 4 * cap_pair - 1),
+        jnp.clip(here, 0, 4 * cap_y - 1),
+        jnp.clip(there, 0, 4 * cap_y - 1),
+        jnp.clip(keep, 0, 8 * cap_pair - 1),
         jnp.clip(job_left, 0, cap_left - 1),
         jnp.clip(job_tile, 0, 4 * cap_x - 1),
         jnp.where(valid, jnp.clip(last, -1, most_jobs - 1), -1),
@@ -280,14 +298,14 @@
 
 
 def spread_part(
-    cap, tv, idx, sections, plan,
+    cap, tv, idx, sections, pick, sender,
     strips, cand, lists,
     left_out, left_in, right_out, row_out,
-    s_idx, r_idx, s_left, r_left, s_right, r_right, s_core, r_core, s_list, r_list, s_row, r_row,
-    meet, on_lists, on_strips,
+    s_idx, r_idx, s_left, r_left, s_right, r_right, s_list, r_list, s_row, r_row,
+    meet, on_lists, on_right, on_strips,
 ):
     r, c = lax.axis_index("row"), lax.axis_index("col")
-    core, y, z = r % 2, c // 2, c % 2
+    y, z = c // 2, c % 2
     for i in range(2):
         for s in range(SECTIONS):
             source = sections[s] // 2
@@ -299,16 +317,16 @@
 
     def pack(yd, _):
         for m in range(cap):
-            right_out[yd, m] = tv[plan[PICKS + yd * (cap + 1) + m]]
+            right_out[yd, m] = tv[pick(yd, m)]
         return 0
 
     lax.fori_loop(0, 4, pack, 0)
     lists[r, c] = idx[...]
     left_in[c] = left_out[c]
-    cand[core, y] = right_out[y]
+    cand[y] = right_out[y]
     meet()
 
-    idx_copies, left_copies, right_copies, core_copies = [], [], [], []
+    idx_copies, left_copies, right_copies = [], [], []
     for d in range(1, COLS):
         to = (c + d) % COLS
         copy = pltpu.make_async_remote_copy(
@@ -327,21 +345,11 @@
     for d in (2, 1, 3):
         to = (y + d) % 4
         copy = pltpu.make_async_remote_copy(
-            right_out.at[to], cand.at[core, y], s_right.at[d], r_right.at[d],
+            right_out.at[to], cand.at[y], s_right.at[d], r_right.at[d],
             device_id={"col": to * 2 + z}, device_id_type=MESH,
         )
         copy.start()
-        right_copies.append((d, copy))
-
-    def to_core(src, origin, d):
-        copy = pltpu.make_async_remote_copy(
-            src, cand.at[core, origin], s_core.at[d], r_core.at[d],
-            device_id={"row": r + 1 - 2 * core}, device_id_type=MESH,
-        )
-        copy.start()
-        core_copies.append(copy)
-
-    to_core(right_out.at[y], y, 0)
+        right_copies.append(copy)
     for copy in idx_copies:
         copy.wait_recv()
     list_copies = []
@@ -357,7 +365,7 @@
         copy.wait_recv()
 
     def reorder(t, _):
-        j = plan[SEND + t]
+        j = sender(t)
         for e in range(ENTRIES):
             row_out[t, e] = left_in[j // 2, (j % 2) * ENTRIES + e]
         return 0
@@ -376,17 +384,13 @@
     for copy in list_copies:
         copy.wait_recv()
     on_lists()
+    for copy in right_copies:
+        copy.wait_recv()
+    on_right()
     for copy in row_copies:
         copy.wait_recv()
     on_strips()
-    for d, copy in right_copies:
-        copy.wait_recv()
-        origin = (y + 4 - d) % 4
-        to_core(cand.at[core, origin], origin, d)
-    for copy in core_copies:
-        copy.wait_recv()
-    sent = [copy for _, copy in right_copies]
-    return idx_copies + left_copies + sent + core_copies + list_copies + row_copies
+    return idx_copies + left_copies + right_copies + list_copies + row_copies
 
 
 def greet(r, c):
@@ -406,8 +410,10 @@
 def spread_kernel(cap, tv, idx, sections, plan, strips, cand, lists, *scratch):
     greet(lax.axis_index("row"), lax.axis_index("col"))
     nothing = lambda: None
+    pick = lambda yd, m: plan[PICKS + yd * (cap + 1) + m]
+    sender = lambda t: plan[SEND + t]
     started = spread_part(
-        cap, tv, idx, sections, plan, strips, cand, lists, *scratch, meet, nothing, nothing
+        cap, tv, idx, sections, pick, sender, strips, cand, lists, *scratch, meet, *[nothing] * 3
     )
     for copy in started:
         copy.wait_send()
@@ -423,7 +429,7 @@
             pltpu.VMEM((4, cap, TILE, TILE), bf),
             pltpu.VMEM((ROWS, ENTRIES, STRIP, TILE), bf),
         ]
-        + [dma((COLS,))] * 8
+        + [dma((COLS,))] * 6
         + [dma((ROWS,))] * 4
     )
 
@@ -434,7 +440,7 @@
         functools.partial(spread_kernel, cap),
         out_shape=(
             jax.ShapeDtypeStruct((ROWS, ENTRIES, STRIP, TILE), bf),
-            jax.ShapeDtypeStruct((2, 4, cap, TILE, TILE), bf),
+            jax.ShapeDtypeStruct((4, cap, TILE, TILE), bf),
             jax.ShapeDtypeStruct((ROWS, COLS, 1, TILE), jnp.int32),
         ),
         in_specs=[VMEM, VMEM, SMEM, SMEM],
@@ -474,13 +480,10 @@
 
 
 def lists_kernel(
-    caps, lists, owner, sections, plan, made, blank,
-    zeros, row_left, inner_left, start, count, col_right, zero_sem,
+    caps, lists, owner, sections, plan, made,
+    row_left, inner_left, start, count, col_right,
 ):
     cap_y, cap_left, cap_pair, cap_x, jobs = caps
-    zeros[...] = jnp.zeros_like(zeros)
-    for p in range(ROWS):
-        pltpu.make_async_copy(zeros, blank.at[pl.ds(p * TILE, TILE)], zero_sem.at[p]).start()
     part = {name: Part(made, base) for name, base in places(caps)[0].items()}
     keep_left, here, there, keep = part["left"], part["here"], part["there"], part["keep"]
     job_left, job_right = part["job_left"], part["job_right"]
@@ -488,7 +491,7 @@
     out_of, slot_of = part["out"], part["slot"]
     row_from, panel_from = Part(plan, ROW_FROM), Part(plan, PANEL_FROM)
     r, c = lax.axis_index("row"), lax.axis_index("col")
-    x, zh = r >> 2, (r >> 1) & 1
+    x = r >> 2
     y, zl = c >> 1, c & 1
     secs = [sections[0], sections[1]]
     for m in range(cap_pair):
@@ -525,41 +528,31 @@
         swap = (b < a).astype(jnp.int32)
         return ((swap, jnp.minimum(a, b)), (1 - swap, jnp.maximum(a, b)))
 
-    def pairs(k2, carry):
-        n_here, n_there = carry
-        g = x * 4 + zh * 2 + k2
-        used = jnp.int32(0)
-        before = jnp.int32(-1)
-        for s, j in ordered(g):
-            source = j >> 1
-            used = jnp.where(source == before, used, 0)
-            before = source
-            line = g * COLS + source
-            base = (j & 1) * BLOCK_COLS
-            near = (source & 1) == zl
-            spot = k2 * 4 * cap_y + (source >> 1) * cap_y
-            for z in range(2):
-                mine = zl == z
-                for k in range(KB):
-                    b = y * 2 + z
-                    rel = lists[line, base + b * KB + k] - b * BLOCK_COLS
-                    ok = (rel >= 0) & (rel < SLAB)
-                    take_here = (ok & near & mine).astype(jnp.int32)
-                    take_there = (ok & near & jnp.logical_not(mine)).astype(jnp.int32)
-                    at = jnp.minimum(spot + used, 8 * cap_y - 1)
-                    here[n_here] = at
-                    there[n_there] = at
-                    n_here = n_here + take_here
-                    n_there = n_there + take_there
-                    used = used + ok.astype(jnp.int32)
-        return n_here, n_there
-
-    lax.fori_loop(0, 2, pairs, (jnp.int32(0), jnp.int32(0)))
+    n_here, n_there, used, before = jnp.int32(0), jnp.int32(0), jnp.int32(0), jnp.int32(-1)
+    for s, j in ordered(r):
+        source = j >> 1
+        used = jnp.where(source == before, used, 0)
+        before = source
+        line = r * COLS + source
+        base = (j & 1) * BLOCK_COLS
+        near = (source & 1) == zl
+        for z in range(2):
+            mine = zl == z
+            for k in range(KB):
+                b = y * 2 + z
+                rel = lists[line, base + b * KB + k] - b * BLOCK_COLS
+                ok = (rel >= 0) & (rel < SLAB)
+                at = jnp.minimum((source >> 1) * cap_y + used, 4 * cap_y - 1)
+                here[n_here] = at
+                there[n_there] = at
+                n_here = n_here + (ok & near & mine).astype(jnp.int32)
+                n_there = n_there + (ok & near & jnp.logical_not(mine)).astype(jnp.int32)
+                used = used + ok.astype(jnp.int32)
 
     def per_x(xs, _):
         def per_zh(zs, n):
             def per_core(k2, carry):
-                n, seen0, seen1 = carry
+                n, seen0, seen1 = carry, jnp.int32(0), jnp.int32(0)
                 g = xs * 4 + zs * 2 + k2
                 for s, j in ordered(g):
                     source = j >> 1
@@ -573,7 +566,8 @@
                         rel = lists[line, base + k] - c * BLOCK_COLS
                         take = ((rel >= 0) & (rel < SLAB)).astype(jnp.int32)
                         seen = jnp.where(odd == 0, seen0, seen1)
-                        at = jnp.minimum((zs * 2 + odd) * cap_pair + seen, 4 * cap_pair - 1)
+                        at = ((zs * 2 + odd) * 2 + k2) * cap_pair
+                        at = jnp.minimum(at + seen, 8 * cap_pair - 1)
                         col_right[xs * (cap_x + 1) + n] = rel
                         keep[jnp.where(xs == x, n, cap_x)] = at
                         n = n + take
@@ -581,9 +575,9 @@
                         seen1 = seen1 + take * odd
                     start[q] = xs * (cap_x + 1) + first
                     count[q] = n - first
-                return n, seen0, seen1
-
-            return lax.fori_loop(0, 2, per_core, (n, jnp.int32(0), jnp.int32(0)))[0]
+                return n
+
+            return lax.fori_loop(0, 2, per_core, n)
 
         lax.fori_loop(0, 2, per_zh, jnp.int32(0))
         return 0
@@ -634,8 +628,6 @@
 
     _, touched = lax.fori_loop(0, left_count, per_left, (jnp.int32(0), jnp.int32(0)))
     part["touched"][0] = touched
-    for p in range(ROWS):
-        pltpu.make_async_copy(zeros, blank.at[pl.ds(p * TILE, TILE)], zero_sem.at[p]).wait()
 
 
 def make_lists(caps, lists, owner, sections, plan):
@@ -643,16 +635,11 @@
     smem = lambda n: pltpu.SMEM((n,), jnp.int32)
     return pl.pallas_call(
         functools.partial(lists_kernel, caps),
-        out_shape=(
-            jax.ShapeDtypeStruct((places(caps)[1],), jnp.int32),
-            jax.ShapeDtypeStruct((ROWS * TILE, SLAB * TILE), jnp.bfloat16),
-        ),
+        out_shape=jax.ShapeDtypeStruct((places(caps)[1],), jnp.int32),
         in_specs=[SMEM] * 4,
-        out_specs=(SMEM, ANY),
+        out_specs=SMEM,
         scratch_shapes=[
-            pltpu.VMEM((TILE, SLAB * TILE), jnp.bfloat16),
             smem(cap_left + 8), smem(cap_left + 8), smem(PANEL), smem(PANEL), smem(4 * (cap_x + 1)),
-            pltpu.SemaphoreType.DMA((ROWS,)),
         ],
         compiler_params=params(4),
     )(lists, owner, sections, plan)
@@ -665,25 +652,22 @@
     cap_y, cap_left, cap_pair, cap_x, jobs = caps
     r, c = lax.axis_index("row"), lax.axis_index("col")
     k = r % 2
-    x, y = r // 4, c // 2
+    x = r // 4
     me = ((r // 2) % 2) * 2 + c % 2
     cz = c + 1 - 2 * (c % 2)
     rz = (r // 4) * 4 + (r + 2) % 4
-    cut = cap_left * 11 // 14
     zp, zh, zx = {"col": cz}, {"row": rz}, {"row": rz, "col": cz}
     yn, yb = {"col": (c + 2) % COLS}, {"col": (c + COLS - 2) % COLS}
     core = {"row": r + 1 - 2 * k}
     xn, xb = {"row": (r + 4) % ROWS}, {"row": (r + ROWS - 4) % ROWS}
-    half, part = cap_pair // 2, cap_x // 2
-
-    def pack_left(m, _):
-        for u in range(4):
-            e = keep_left[m * 4 + u]
-            left[c, m * 4 + u] = strips[e // ENTRIES, e % ENTRIES]
-        return 0
-
-    lax.fori_loop(0, cap_left // 4, pack_left, 0)
-
+    part = cap_x // 2
+    end = cap_left
+    mid = end // 2
+    c_m, c_p = (c + COLS - 2) % COLS, (c + 2) % COLS
+    z_m, z_p = (cz + COLS - 2) % COLS, (cz + 2) % COLS
+    x_m, x_p, x_o = (x + 3) % 4, (x + 1) % 4, (x + 2) % 4
+    z_of_p, z_of_h = (me // 2) * 2 + (me + 1) % 2, (me + 2) % 4
+    z_of_x = (z_of_p + 2) % 4
     started, done = [], []
 
     def push(src, dst, to):
@@ -699,66 +683,60 @@
         piece = left.at[origin, pl.ds(a, b - a)]
         return push(piece, piece, to)
 
+    def gz(origin, to):
+        piece = held.at[origin, k]
+        return push(piece, piece, to)
+
     def gx(origin, a, b, to):
         piece = right.at[origin, k, pl.ds(a, b - a)]
         return push(piece, piece, to)
 
-    def arrived(copy):
-        copy.wait_recv()
-        done.append(copy)
-
-    end = cap_left
-    a_mid, b_mid = cut // 2, (cut + end) // 2
-    c_m, c_p, c_o = (c + COLS - 2) % COLS, (c + 2) % COLS, (c + 4) % COLS
-    z_m, z_p = (cz + COLS - 2) % COLS, (cz + 2) % COLS
-    x_m, x_p, x_o = (x + 3) % 4, (x + 1) % 4, (x + 2) % 4
-    z_of_p, z_of_h = (me // 2) * 2 + (me + 1) % 2, (me + 2) % 4
-    z_of_x = (z_of_p + 2) % 4
-
-    k1 = go(c, 0, cut, zp)
-    k2 = go(c, 0, cut, yn)
-    k3 = go(c, 0, cut, yb)
-    k10 = go(c, cut, end, yn)
-    k11 = go(c, cut, end, yb)
-    k12 = go(c, cut, end, zp)
-    yield
-    for m in range(half):
-        e = there[k * half + m]
-        other[m] = cand[e // (4 * cap_y), (e // cap_y) % 4, e % cap_y]
+    def arrived(*copies):
+        for copy in copies:
+            copy.wait_recv()
+            done.append(copy)
+
     for m in range(cap_pair):
+        e = there[m]
+        other[m] = cand[e // cap_y, e % cap_y]
         e = here[m]
-        held[me, m // half, m % half] = cand[e // (4 * cap_y), (e // cap_y) % 4, e % cap_y]
-
+        held[me, k, m] = cand[e // cap_y, e % cap_y]
     s1 = push(other, held.at[me, k], zp)
     s2 = push(other, held.at[me, k], zx)
-    s3 = push(held.at[me, k], held.at[me, k], zh)
+    s3 = gz(me, zh)
+    t0 = gz(me, core)
+    yield started
+
+    def pack_left(m, _):
+        for u in range(4):
+            e = keep_left[m * 4 + u]
+            left[c, m * 4 + u] = strips[e // ENTRIES, e % ENTRIES]
+        return 0
+
+    lax.fori_loop(0, cap_left // 4, pack_left, 0)
+    k1 = go(c, 0, end, zp)
+    k2 = go(c, 0, end, yn)
+    k3 = go(c, 0, end, yb)
+    yield started
     arrived(s1)
-    t1 = push(held.at[z_of_p, k], held.at[z_of_p, k], core)
+    t1 = gz(z_of_p, core)
     arrived(s2)
-    t2 = push(held.at[z_of_x, k], held.at[z_of_x, k], core)
+    t2 = gz(z_of_x, core)
     arrived(s3)
-    t3 = push(held.at[z_of_h, k], held.at[z_of_h, k], core)
-    arrived(k2)
-    k6 = go(c_m, 0, a_mid, yn)
-    arrived(k3)
-    k7 = go(c_p, a_mid, cut, yb)
-    arrived(k1)
-    k4 = go(cz, 0, cut, yn)
-    k5 = go(cz, 0, cut, yb)
-    arrived(t1)
-    arrived(t2)
-    arrived(t3)
+    t3 = gz(z_of_h, core)
+    arrived(t0, t1, t2, t3)
     for m in range(cap_x):
         e = keep[m]
-        right[x, m // part, m % part] = held[e // cap_pair, (e // half) % 2, e % half]
+        right[x, m // part, m % part] = held[e // (2 * cap_pair), (e // cap_pair) % 2, e % cap_pair]
     u1 = gx(x, 0, part, xn)
     u2 = gx(x, 0, part, xb)
-    arrived(k10)
-    k13 = go(c_m, cut, b_mid, yn)
-    k14 = go(c_m, cut, end, zp)
-    arrived(k11)
-    k15 = go(c_p, b_mid, end, yb)
-    k16 = go(c_p, cut, end, zp)
+    arrived(k1)
+    k4 = go(cz, 0, end, yn)
+    k5 = go(cz, 0, end, yb)
+    arrived(k2)
+    k6 = go(c_m, 0, mid, yn)
+    arrived(k3)
+    k7 = go(c_p, mid, end, yb)
     arrived(u1)
     u3 = gx(x_m, 0, part // 2, xn)
     u4 = gx(x_m, 0, part, core)
@@ -766,13 +744,9 @@
     u5 = gx(x_p, part // 2, part, xb)
     u6 = gx(x_p, 0, part, core)
     arrived(k4)
-    k8 = go(z_m, 0, a_mid, yn)
+    k8 = go(z_m, 0, mid, yn)
     arrived(k5)
-    k9 = go(z_p, a_mid, cut, yb)
-    arrived(k13)
-    k17 = go(c_o, cut, b_mid, zp)
-    arrived(k15)
-    k18 = go(c_o, b_mid, end, zp)
+    k9 = go(z_p, mid, end, yb)
     arrived(u3)
     u7 = gx(x_o, 0, part // 2, core)
     arrived(u5)
@@ -841,7 +815,8 @@
         caps, found["left"], found["here"], found["there"], found["keep"],
         strips, cand, left, right, held, other, send, recv,
     )
-    next(steps)
+    for _ in range(2):
+        next(steps)
     started = next(steps)
     started += product_part(
         caps, found["job_left"], found["job_right"], found["job_last"], found["job_col"],
@@ -851,7 +826,7 @@
         copy.wait_send()
 
 
-COPIES = 32
+COPIES = 24
 
 
 def multiply_scratch(caps):
@@ -862,8 +837,8 @@
         [
             pltpu.VMEM((COLS, cap_left, STRIP, TILE), bf),
             pltpu.VMEM((4, 2, cap_x // 2, TILE, TILE), bf),
-            pltpu.VMEM((4, 2, cap_pair // 2, TILE, TILE), bf),
-            pltpu.VMEM((cap_pair // 2, TILE, TILE), bf),
+            pltpu.VMEM((4, 2, cap_pair, TILE, TILE), bf),
+            pltpu.VMEM((cap_pair, TILE, TILE), bf),
             pltpu.VMEM((ROWS, TILE), f32),
             pltpu.VMEM((ROWS, ROWS, TILE), f32),
         ]
@@ -888,6 +863,36 @@
     )(strips, cand, plan)
 
 
+def vector_prep(cap_y, owner, idx, sections, r, c):
+    i32 = jnp.int32
+    line = lax.broadcasted_iota(i32, (ROWS, TILE), 0)
+    lane = lax.broadcasted_iota(i32, (ROWS, TILE), 1)
+    blocks = [jnp.broadcast_to(owner[h : h + 1, :] >> 4, (ROWS, TILE)) for h in range(2)]
+    who = jnp.zeros((ROWS, 1), i32)
+    own = [jnp.zeros((ROWS, 1), i32) for _ in range(2)]
+    for h in range(2):
+        t = lane + h * TILE
+        hit = (blocks[h] == line) & ((t >> 4) == r)
+        who = who + jnp.where(hit, lane & (ROWS - 1), 0).sum(axis=1, keepdims=True)
+        for i in range(2):
+            hit = t == r * ROWS + c * 2 + i
+            own[i] = own[i] + jnp.where(hit, blocks[h], 0).sum(axis=1, keepdims=True)
+    sec0, sec1 = sections[0], sections[1]
+    mine = jnp.where(lane < BLOCK_COLS, own[0], own[1])
+    b = (lane & (BLOCK_COLS - 1)) >> 2
+    rel = jnp.broadcast_to(idx[...], (ROWS, TILE)) - b * BLOCK_COLS
+    ok = (lane < 2 * BLOCK_COLS) & (rel >= 0) & (rel < SLAB) & ((mine == sec0) | (mine == sec1))
+    ok = ok & ((b >> 1) == line)
+    rank = mm(picked(ok), picked(iota(0) < iota(1))).astype(i32)
+    rank = jnp.where(ok, rank, -1)
+    plan = jnp.where(lane == TILE - 1, jnp.clip(who, 0, ROWS - 1), 0)
+    for m in range(cap_y):
+        at = jnp.where(rank == m, lane, 0).sum(axis=1, keepdims=True)
+        at = jnp.clip(at, 0, 2 * BLOCK_COLS - 1)
+        plan = jnp.where(lane == m, at, plan)
+    return plan
+
+
 class Row:
     def __init__(self, ref, row):
         self.ref, self.row = ref, row
@@ -897,18 +902,20 @@
 
 
 def whole_kernel(
-    caps, tv, idx, owner, sections, plan,
-    sums, totals, blank, made, over,
-    strips, cand, lists, zeros, scalars, zero_sem, plan_sem, *scratch,
+    caps, values, idx, owner, sections,
+    sums, totals, made, over,
+    tv, strips, cand, lists, early, places_of, scalars, value_sem, plan_sem, *scratch,
 ):
     r, c = lax.axis_index("row"), lax.axis_index("col")
     greet(r, c)
-    zeros[...] = jnp.zeros_like(zeros)
-    clears = [
-        pltpu.make_async_copy(zeros, blank.at[pl.ds(p * TILE, TILE)], zero_sem.at[p])
-        for p in range(ROWS)
-    ]
-    first, second = scratch[:16], scratch[16:]
+    load = pltpu.make_async_copy(values, tv, value_sem)
+    load.start()
+    early[...] = vector_prep(caps[0], owner, idx, sections, r, c)
+    move = pltpu.make_async_copy(early, places_of, plan_sem)
+    move.start()
+    move.wait()
+    load.wait()
+    first, second = scratch[:14], scratch[14:]
     left, right, held, other, rows, parts, send, recv, total_send, total_recv = second
     row = lambda n: Row(scalars, n)
     steps = gather_part(
@@ -922,13 +929,13 @@
         over[...] = excess
         move = pltpu.make_async_copy(made, scalars, plan_sem)
         move.start()
-        for copy in clears:
-            copy.start()
         move.wait()
 
     started = spread_part(
-        caps[0], tv, idx, sections, plan, strips, cand, lists, *first,
-        meet, on_lists, lambda: next(steps),
+        caps[0], tv, idx, sections,
+        lambda yd, m: places_of[yd, m], lambda t: places_of[t, TILE - 1],
+        strips, cand, lists, *first,
+        meet, on_lists, *[lambda: next(steps)] * 2,
     )
     started = started + next(steps)
     started += product_part(
@@ -937,11 +944,9 @@
     )
     for copy in started:
         copy.wait_send()
-    for copy in clears:
-        copy.wait()
-
-
-def whole(caps, collective_id, tv, idx, owner, sections, plan):
+
+
+def whole(caps, collective_id, tv, idx, owner, sections):
     bf, f32, i32 = jnp.bfloat16, jnp.float32, jnp.int32
     dma = pltpu.SemaphoreType.DMA
     return pl.pallas_call(
@@ -949,78 +954,99 @@
         out_shape=(
             jax.ShapeDtypeStruct((caps[4], TILE, TILE), f32),
             jax.ShapeDtypeStruct((ROWS, TILE), f32),
-            jax.ShapeDtypeStruct((ROWS * TILE, SLAB * TILE), bf),
             jax.ShapeDtypeStruct((ROWS, TILE), i32),
             jax.ShapeDtypeStruct((TILE, TILE), f32),
         ),
-        in_specs=[VMEM, VMEM, VMEM, SMEM, SMEM],
-        out_specs=(VMEM, VMEM, ANY, VMEM, VMEM),
+        in_specs=[HBM, VMEM, VMEM, SMEM],
+        out_specs=(VMEM,) * 4,
         scratch_shapes=[
+            pltpu.VMEM((2 * COLS * KB, TILE, TILE), bf),
             pltpu.VMEM((ROWS, ENTRIES, STRIP, TILE), bf),
-            pltpu.VMEM((2, 4, caps[0], TILE, TILE), bf),
+            pltpu.VMEM((4, caps[0], TILE, TILE), bf),
             pltpu.VMEM((ROWS, COLS, 1, TILE), i32),
-            pltpu.VMEM((TILE, SLAB * TILE), bf),
+            pltpu.VMEM((ROWS, TILE), i32),
             pltpu.SMEM((ROWS, TILE), i32),
-            dma((ROWS,)),
+            pltpu.SMEM((ROWS, TILE), i32),
+            dma,
             dma,
         ]
         + spread_scratch(caps[0])
         + multiply_scratch(caps),
-        compiler_params=params(40, collective_id=collective_id, has_side_effects=True),
-    )(tv, idx, owner, sections, plan)
-
-
-def write_listed_kernel(jobs, sums, blank, plan, totals, out, block, factor, out_sem):
+        compiler_params=params(24, collective_id=collective_id, has_side_effects=True),
+    )(tv, idx, owner, sections)
+
+
+def write_listed_kernel(jobs, sums, plan, totals, out, block, factor, zeros, zero_sem, out_sem):
+    zeros[...] = jnp.zeros_like(zeros)
+    clears = [
+        pltpu.make_async_copy(zeros, out.at[pl.ds(p * TILE, TILE)], zero_sem.at[p])
+        for p in range(ROWS)
+    ]
+    for copy in clears:
+        copy.start()
     count = float(ROWS * ROWS * TILE)
     factor[...] = count / (totals[...] + 1e-06)
 
-    def place(n):
+    def scale(n, _):
         o = plan[ROW_OUT, n]
-        p = jnp.maximum(o, 0) // SLAB
-        col = jnp.maximum(o, 0) - p * SLAB
-        row = pl.ds(pl.multiple_of(p * TILE, TILE), TILE)
-        lanes = pl.ds(pl.multiple_of(col * TILE, TILE), TILE)
-        return o, col, pltpu.make_async_copy(block.at[n], out.at[row, lanes], out_sem)
-
-    def scale(n, _):
-        o, col, copy = place(n)
 
         @pl.when(o >= 0)
         def _():
             value = sums[n]
+            col = o - o // SLAB * SLAB
             block[n] = (value * value * factor[pl.ds(col, 1), :]).astype(jnp.bfloat16)
-            copy.start()
 
         return 0
 
     lax.fori_loop(0, jobs, scale, 0)
-
-    def drain(n, _):
-        o, _, copy = place(n)
+    for copy in clears:
+        copy.wait()
+
+    def place(n, o):
+        p = o // SLAB
+        col = o - p * SLAB
+        row = pl.ds(pl.multiple_of(p * TILE, TILE), TILE)
+        lanes = pl.ds(pl.multiple_of(col * TILE, TILE), TILE)
+        return pltpu.make_async_copy(block.at[n], out.at[row, lanes], out_sem)
+
+    def send(n, _):
+        o = plan[ROW_OUT, n]
 
         @pl.when(o >= 0)
         def _():
-            copy.wait()
+            place(n, o).start()
+
+        return 0
+
+    lax.fori_loop(0, jobs, send, 0)
+
+    def drain(n, _):
+        o = plan[ROW_OUT, n]
+
+        @pl.when(o >= 0)
+        def _():
+            place(n, o).wait()
 
         return 0
 
     lax.fori_loop(0, jobs, drain, 0)
 
 
-def write_listed(jobs, sums, blank, plan, totals):
+def write_listed(jobs, sums, plan, totals):
     return pl.pallas_call(
         functools.partial(write_listed_kernel, jobs),
         out_shape=jax.ShapeDtypeStruct((ROWS * TILE, SLAB * TILE), jnp.bfloat16),
-        in_specs=[VMEM, ANY, SMEM, VMEM],
+        in_specs=[VMEM, SMEM, VMEM],
         out_specs=ANY,
-        input_output_aliases={1: 0},
         scratch_shapes=[
             pltpu.VMEM((jobs, TILE, TILE), jnp.bfloat16),
             pltpu.VMEM((ROWS, TILE), jnp.float32),
+            pltpu.VMEM((TILE, SLAB * TILE), jnp.bfloat16),
+            pltpu.SemaphoreType.DMA((ROWS,)),
             pltpu.SemaphoreType.DMA,
         ],
         compiler_params=params(12),
-    )(sums, blank, plan, totals)
+    )(sums, plan, totals)
 
 
 def write_kernel(at, sums, blank, plan, totals, out, block, factor, out_sem):
@@ -1076,22 +1102,18 @@
     tv = tile_values.reshape(2 * COLS * KB, TILE, TILE)
     owner_rows = owner_map.reshape(2, TILE)
 
-    def full():
-        plan = prep(FULL[0], owner_map, section_rows, flat)
+    sums, totals, made, over = whole(FAST, 0, tv, idx, owner_rows, section_rows)
+
+    out = write_listed(FAST[4], sums, made, totals)
+
+    def full(state):
+        plan, blank = prep(FULL[0], owner_map, section_rows, flat)
         strips, cand, lists = spread(FULL[0], 2, tv, idx, section_rows, plan)
-        made, blank = make_lists(
-            FULL, lists.reshape(ROWS * COLS, TILE), owner_map, section_rows, plan
-        )
+        made = make_lists(FULL, lists.reshape(ROWS * COLS, TILE), owner_map, section_rows, plan)
         sums, totals = multiply(FULL, 3, strips, cand, made)
-        return write(FULL, sums, blank, made, totals)
-
-    plan = prep(FAST[0], owner_map, section_rows, flat)
-    *got, over = whole(FAST, 0, tv, idx, owner_rows, section_rows, plan)
-
-    def packed(sums, totals, blank, made):
-        return write_listed(FAST[4], sums, blank, made, totals)
-
-    return lax.cond(jnp.max(over) > 0, lambda *_: full(), packed, *got)
+        return jnp.float32(0), write(FULL, sums, blank, made, totals)
+
+    return lax.while_loop(lambda state: state[0] > 0, full, (jnp.max(over), out))[1]
 
 
 def solution(mesh):

time: 91.1 us -> 75.3 us (0.83)
  Pallas kernels: 81.6 us -> 72.9 us
  local copies, waits for them, and re-layouts: 7.4 us -> 0.88 us
    pallas_call x1, Pallas kernels: 74.1 us -> 67.3 us  [whole(): pl.pallas_call(functools.partial(whole_kernel, caps), out_shape=(jax.Shap...]
    unnamed x4 -> x7, local copies, waits for them, and re-layouts: 7.31 us -> 0.79 us
    pallas_call x1 -> x0, Pallas kernels: 1.97 us -> none  [prep(): pl.pallas_call(functools.partial(prep_kernel, cap), out_shape=jax.ShapeDt...]
where the time goes in v1:
time: 75.3 us; the launch traced here: 75.1 us
  Pallas kernels  72.9 us (97%)
  local copies, waits for them, and re-layouts  0.88 us (1%)
    pallas_call x1, Pallas kernels, whole(): pl.pallas_call(functools.partial(whole_kernel, caps), out_shape=(jax.Shap...  67.3 us
    pallas_call x1, Pallas kernels, write_listed(): pl.pallas_call(functools.partial(write_listed_kernel, jobs), out_shape=ja...  5.62 us

profile of v1, /device:TPU:1, one launch (start us, length us, event | category | flops | bytes accessed | tf_op | source)
XLA Modules:
  0.0 75.1 jit_solution(2268728993485569166)
XLA Ops:
  0.0 0.8 %copy.7 = s32[2,8,4]{2,1,0:T(8,128)S(1)} copy(s32[2,8,4]{1,2,0:T(4,128)} %param.7) | data formatting | bytes 512 | tf_op args[1]
  0.8 0.1 reshape.16
  0.9 67.3 %shard_map.46 = (f32[80,128,128]{2,1,0:T(8,128)S(1)}, f32[16,128]{1,0:T(8,128)S(1)}, s32[16,128]{1,0:T(8,128)S(1)}, f32[128,128]{1,0:T(8,128)S(1)}) custom-call(bf16[64,128,128]{2,1,0:T(8,128)(2,1)} %bitcast.6, s32[1,128]{1,0:T(1,128)S(1)} %pad_bitcast_fusion.idx, s32[2,128]{1,0:T(2,128)} %bitcast.8, s32[2]{0:T(128)} %sections.1), custom_call_target="tpu_custom_call" | custom-call | tf_op jit(solution)/shard_map/pallas_call | solution.py:952
  68.1 0.0 copy-start.5
  68.2 0.0 copy-start.6
  68.2 0.0 copy-start.7
  68.2 5.6 %shard_map.47 = bf16[2048,1536]{1,0:T(8,128)(2,1)} custom-call(f32[80,128,128]{2,1,0:T(8,128)S(1)} %get-tuple-element.52.sums, s32[16,128]{1,0:T(8,128)S(1)} %get-tuple-element.53.plan, f32[16,128]{1,0:T(8,128)S(1)} %get-tuple-element.54.totals), custom_call_target="tpu_custom_call" | custom-call | tf_op jit(solution)/shard_map/pallas_call | solution.py:1036
  73.8 0.7 reduce_max.9
  74.5 0.0 copy-done.5
  74.5 0.0 copy-done.6
  74.5 0.0 copy-done.7
  74.5 0.6 while.9
  (1 shorter events, 0.0 us)
Async XLA Ops:
  68.1 6.3 %copy-start.5 = (bf16[2,8,4,128,128]{4,3,2,1,0:T(8,128)(2,1)S(1)}, bf16[2,8,4,128,128]{4,3,2,1,0:T(8,128)(2,1)}, u32[]{:S(2)}) copy-start(bf16[2,8,4,128,128]{4,3,2,1,0:T(8,128)(2,1)} %param.6) | copy-start | bytes 6291460
  68.2 6.3 %copy-start.6 = (s32[2]{0:T(128)S(1)}, s32[2]{0:T(128)}, u32[]{:S(2)}) copy-start(s32[2]{0:T(128)} %sections.1) | copy-start | bytes 28
  68.2 6.3 %copy-start.7 = (s32[256]{0:T(256)S(1)}, s32[256]{0:T(256)}, u32[]{:S(2)}) copy-start(s32[256]{0:T(256)} %param.8) | copy-start | bytes 3076

commit v2 on v1

--- a/solution.py
+++ b/solution.py
@@ -17,7 +17,7 @@
 STRIP = TILE // COLS
 ENTRIES = SECTIONS * KB
 PANEL = SECTIONS * ROWS
-FAST = (8, 56, 6, 16, 80)
+FAST = (9, 60, 7, 16, 96)
 FULL = (16, 128, 8, 32, 512)
 MESH = pl.DeviceIdType.MESH
 VMEM = pl.BlockSpec(memory_space=pltpu.VMEM)
@@ -407,8 +407,11 @@
     pl.semaphore_wait(pltpu.get_barrier_semaphore(), COLS - 1 + ROWS - 1 + 1)
 
 
-def spread_kernel(cap, tv, idx, sections, plan, strips, cand, lists, *scratch):
+def spread_kernel(cap, values, idx, sections, plan, strips, cand, lists, tv, value_sem, *scratch):
     greet(lax.axis_index("row"), lax.axis_index("col"))
+    load = pltpu.make_async_copy(values, tv, value_sem)
+    load.start()
+    load.wait()
     nothing = lambda: None
     pick = lambda yd, m: plan[PICKS + yd * (cap + 1) + m]
     sender = lambda t: plan[SEND + t]
@@ -443,9 +446,10 @@
             jax.ShapeDtypeStruct((4, cap, TILE, TILE), bf),
             jax.ShapeDtypeStruct((ROWS, COLS, 1, TILE), jnp.int32),
         ),
-        in_specs=[VMEM, VMEM, SMEM, SMEM],
+        in_specs=[HBM, VMEM, SMEM, SMEM],
         out_specs=(VMEM,) * 3,
-        scratch_shapes=spread_scratch(cap),
+        scratch_shapes=[pltpu.VMEM((2 * COLS * KB, TILE, TILE), bf), pltpu.SemaphoreType.DMA]
+        + spread_scratch(cap),
         compiler_params=params(20, collective_id=collective_id, has_side_effects=True),
     )(tv, idx, sections, plan)
 
@@ -714,9 +718,12 @@
         return 0
 
     lax.fori_loop(0, cap_left // 4, pack_left, 0)
-    k1 = go(c, 0, end, zp)
-    k2 = go(c, 0, end, yn)
-    k3 = go(c, 0, end, yb)
+    k1a = go(c, 0, mid, zp)
+    k2a = go(c, 0, mid, yn)
+    k3b = go(c, mid, end, yb)
+    k1b = go(c, mid, end, zp)
+    k2b = go(c, mid, end, yn)
+    k3a = go(c, 0, mid, yb)
     yield started
     arrived(s1)
     t1 = gz(z_of_p, core)
@@ -728,29 +735,39 @@
     for m in range(cap_x):
         e = keep[m]
         right[x, m // part, m % part] = held[e // (2 * cap_pair), (e // cap_pair) % 2, e % cap_pair]
-    u1 = gx(x, 0, part, xn)
-    u2 = gx(x, 0, part, xb)
-    arrived(k1)
-    k4 = go(cz, 0, end, yn)
-    k5 = go(cz, 0, end, yb)
-    arrived(k2)
+    h = part // 2
+    u1a = gx(x, 0, h, xn)
+    u2b = gx(x, h, part, xb)
+    u1b = gx(x, h, part, xn)
+    u2a = gx(x, 0, h, xb)
+    arrived(k2a)
     k6 = go(c_m, 0, mid, yn)
-    arrived(k3)
+    arrived(k3b)
     k7 = go(c_p, mid, end, yb)
-    arrived(u1)
-    u3 = gx(x_m, 0, part // 2, xn)
-    u4 = gx(x_m, 0, part, core)
-    arrived(u2)
-    u5 = gx(x_p, part // 2, part, xb)
-    u6 = gx(x_p, 0, part, core)
-    arrived(k4)
+    arrived(k1a)
+    k4a = go(cz, 0, mid, yn)
+    arrived(k1b)
+    k5b = go(cz, mid, end, yb)
+    k4b = go(cz, mid, end, yn)
+    k5a = go(cz, 0, mid, yb)
+    arrived(u1a)
+    u3 = gx(x_m, 0, h, xn)
+    u4a = gx(x_m, 0, h, core)
+    arrived(u2b)
+    u5 = gx(x_p, h, part, xb)
+    u6b = gx(x_p, h, part, core)
+    arrived(k4a)
     k8 = go(z_m, 0, mid, yn)
-    arrived(k5)
+    arrived(k5b)
     k9 = go(z_p, mid, end, yb)
+    arrived(u1b)
+    u4b = gx(x_m, h, part, core)
+    arrived(u2a)
+    u6a = gx(x_p, 0, h, core)
     arrived(u3)
-    u7 = gx(x_o, 0, part // 2, core)
+    u7 = gx(x_o, 0, h, core)
     arrived(u5)
-    u8 = gx(x_o, part // 2, part, core)
+    u8 = gx(x_o, h, part, core)
     for copy in started:
         if not any(copy is seen for seen in done):
             copy.wait_recv()
@@ -826,7 +843,7 @@
         copy.wait_send()
 
 
-COPIES = 24
+COPIES = 33
 
 
 def multiply_scratch(caps):
@@ -926,7 +943,7 @@
     def on_lists():
         found, excess = vector_plan(caps, lists, owner, sections, r, c)
         made[...] = found
-        over[...] = excess
+        over[...] = jnp.broadcast_to(excess.max(axis=0, keepdims=True), (8, TILE))
         move = pltpu.make_async_copy(made, scalars, plan_sem)
         move.start()
         move.wait()
@@ -955,7 +972,7 @@
             jax.ShapeDtypeStruct((caps[4], TILE, TILE), f32),
             jax.ShapeDtypeStruct((ROWS, TILE), f32),
             jax.ShapeDtypeStruct((ROWS, TILE), i32),
-            jax.ShapeDtypeStruct((TILE, TILE), f32),
+            jax.ShapeDtypeStruct((8, TILE), f32),
         ),
         in_specs=[HBM, VMEM, VMEM, SMEM],
         out_specs=(VMEM,) * 4,

time: 75.3 us -> 77 us (1.023)
  Pallas kernels: 72.9 us -> 74.5 us
    pallas_call x1, Pallas kernels: 67.3 us -> 68.4 us  [whole(): pl.pallas_call(functools.partial(whole_kernel, caps), out_shape=(jax.Shap...]
where the time goes in v2:
time: 77 us; the launch traced here: 76.7 us
  Pallas kernels  74.5 us (97%)
  local copies, waits for them, and re-layouts  0.88 us (1%)
    pallas_call x1, Pallas kernels, whole(): pl.pallas_call(functools.partial(whole_kernel, caps), out_shape=(jax.Shap...  68.4 us
    pallas_call x1, Pallas kernels, write_listed(): pl.pallas_call(functools.partial(write_listed_kernel, jobs), out_shape=ja...  6.13 us

profile of v2, /device:TPU:1, one launch (start us, length us, event | category | flops | bytes accessed | tf_op | source)
XLA Modules:
  0.0 76.7 jit_solution(1236118011496082225)
XLA Ops:
  0.0 0.8 copy.7
  0.8 0.1 reshape.16
  0.9 68.4 %shard_map.46 = (f32[96,128,128]{2,1,0:T(8,128)S(1)}, f32[16,128]{1,0:T(8,128)S(1)}, s32[16,128]{1,0:T(8,128)S(1)}, f32[8,128]{1,0:T(8,128)S(1)}) custom-call(bf16[64,128,128]{2,1,0:T(8,128)(2,1)} %bitcast.6, s32[1,128]{1,0:T(1,128)S(1)} %pad_bitcast_fusion.idx, s32[2,128]{1,0:T(2,128)} %bitcast.8, s32[2]{0:T(128)} %sections.1), custom_call_target="tpu_custom_call" | custom-call | tf_op jit(solution)/shard_map/pallas_call | solution.py:969
  69.3 0.0 copy-start.5
  69.3 0.0 copy-start.6
  69.3 0.0 copy-start.7
  69.3 6.1 %shard_map.47 = bf16[2048,1536]{1,0:T(8,128)(2,1)} custom-call(f32[96,128,128]{2,1,0:T(8,128)S(1)} %get-tuple-element.52.sums, s32[16,128]{1,0:T(8,128)S(1)} %get-tuple-element.53.plan, f32[16,128]{1,0:T(8,128)S(1)} %get-tuple-element.54.totals), custom_call_target="tpu_custom_call" | custom-call | tf_op jit(solution)/shard_map/pallas_call | solution.py:1053
  75.4 0.7 reduce_max.9
  76.1 0.0 copy-done.5
  76.1 0.0 copy-done.6
  76.1 0.0 copy-done.7
  76.1 0.6 while.9
  (1 shorter events, 0.0 us)
Async XLA Ops:
  69.3 6.8 %copy-start.5 = (bf16[2,8,4,128,128]{4,3,2,1,0:T(8,128)(2,1)S(1)}, bf16[2,8,4,128,128]{4,3,2,1,0:T(8,128)(2,1)}, u32[]{:S(2)}) copy-start(bf16[2,8,4,128,128]{4,3,2,1,0:T(8,128)(2,1)} %param.6) | copy-start | bytes 6291460
  69.3 6.8 %copy-start.6 = (s32[2]{0:T(128)S(1)}, s32[2]{0:T(128)}, u32[]{:S(2)}) copy-start(s32[2]{0:T(128)} %sections.1) | copy-start | bytes 28
  69.3 6.8 %copy-start.7 = (s32[256]{0:T(256)S(1)}, s32[256]{0:T(256)}, u32[]{:S(2)}) copy-start(s32[256]{0:T(256)} %param.8) | copy-start | bytes 3076
